TPU v7x, 32 devices: a whole 2x2x4 slice. The times are simulated.
32 devices in a mesh: edge: 4 (over y, x), tile: 8 (over z, core).
Axes of the slice: x: 2, y: 2, z: 4, core: 2. Of those that a mesh axis runs over, the one named last changes fastest.
Arguments:
- features: bfloat16 [96, 48, 64, 128], P('edge', 'tile'), may hold values from -6 to 6
- hidden_state: bfloat16 [32, 48, 64, 128], P('edge', 'tile'), may hold values from -1 to 1
- edge_source: int32 [32], P('edge'), may hold values from 0 to 23
- edge_owner: int32 [32, 1], P('edge'), may hold values from 0 to 3; in each aligned block of 8 rows (0 to 7, 8 to 15, ...) at most 4 rows name the same one
- edge_target: int32 [32], P('edge'), may hold values from 0 to 23
- edge_counts: int32 [4], P('edge'), may hold values from 4 to 8, as said below
- corr_weight: bfloat16 [49, 128], replicated, may hold values from -0.875 to 0.875
- gate_weight: bfloat16 [3, 3, 256, 256], replicated, may hold values from -0.125 to 0.125
- candidate_weight: bfloat16 [3, 3, 256, 128], replicated, may hold values from -0.125 to 0.125
- jacobian_weight: bfloat16 [128, 24], replicated, may hold values from -0.5 to 0.5
- confidence_weight: bfloat16 [128, 2], replicated, may hold values from -3 to 3
Outputs:
- hidden_next: bfloat16 [32, 48, 64, 128], P('edge', 'tile')
- camera_hessian: float32 [576, 576], P('tile', 'edge')
- pose_diagonal: float32 [96, 36], P('edge')
Inputs may be any that keep to these rules, and one draw needn't show every extreme that they name: `edge_owner`: in the rows of one index of edge at most 4 edges name the same owner, a bound that some block reaches. `edge_counts`: edges past a device's count are unused; some index of edge uses all 8.
All inputs are finite; a program needn't handle non-finite values.
Results may differ from a plain program's by a relative error of at most 0.015.
Values may be sent and summed in bfloat16 or wider, within the bound.
A program may use at most 128 MiB of HBM per device.

v0:
```python
import jax
import jax.numpy as jnp
from jax import lax
from jax.sharding import PartitionSpec as P

MAPH = 48
MAPW = 64
WINDOW = 7


def padded_2(cells, sides, width):
    for axis, dim in sides:
        count = lax.axis_size(axis)
        ends = count - 1
        head = lax.slice_in_dim(cells, 0, width, axis=dim)
        tail = lax.slice_in_dim(cells, cells.shape[dim] - width, cells.shape[dim], axis=dim)
        cells = jnp.concatenate(
            [
                lax.ppermute(tail, axis, [(i, (i + 1) % count) for i in range(ends)]),
                cells,
                lax.ppermute(head, axis, [((i + 1) % count, i) for i in range(ends)]),
            ],
            axis=dim,
        )
    return cells


def pad_columns(values):
    return jnp.pad(values, ((0, 0), (0, 0), (1, 1), (0, 0)))


def convolve(padded, weight):
    row_count = padded.shape[1] - 2
    col_count = padded.shape[2] - 2
    running = jnp.zeros((padded.shape[0], row_count, col_count, weight.shape[-1]), jnp.float32)
    for row_step in range(3):
        for col_step in range(3):
            window = padded[:, row_step : row_step + row_count, col_step : col_step + col_count]
            running = running + jnp.einsum(
                "erwc,ck->erwk",
                window,
                weight[row_step, col_step],
                preferred_element_type=jnp.float32,
            )
    return running


def per_device(
    features,
    hidden_state,
    edge_source,
    edge_owner,
    edge_target,
    edge_counts,
    corr_weight,
    gate_weight,
    candidate_weight,
    jacobian_weight,
    confidence_weight,
):
    edge_total = hidden_state.shape[0]
    frame_total = features.shape[0]
    band_rows = features.shape[1]
    map_width = features.shape[2]
    hidden_width = hidden_state.shape[3]
    owner_count = lax.axis_size("edge")
    slot_depth = max(2, (2 * edge_total + owner_count - 1) // owner_count)
    my_index = lax.axis_index("edge")
    in_use = jnp.arange(edge_total) < edge_counts[0]
    owners = edge_owner[:, 0]
    owner_hits = (owners[:, None] == jnp.arange(owner_count)[None, :]).astype(jnp.int32)
    earlier = jnp.cumsum(owner_hits, axis=0) - owner_hits
    rank_within = jnp.sum(earlier * owner_hits, axis=1)
    slot_index = owners * slot_depth + rank_within
    slot_hits = (slot_index[:, None] == jnp.arange(owner_count * slot_depth)[None, :]).astype(
        jnp.int32
    )
    source_global = my_index * frame_total + edge_source
    target_global = owners * frame_total + edge_target
    send_target = jnp.sum(slot_hits * edge_target[:, None], axis=0).reshape(owner_count, slot_depth)
    send_source = jnp.sum(slot_hits * source_global[:, None], axis=0).reshape(
        owner_count, slot_depth
    )
    got_target, got_source = (
        lax.all_to_all(send_target, "edge", split_axis=0, concat_axis=0, tiled=True),
        lax.all_to_all(send_source, "edge", split_axis=0, concat_axis=0, tiled=True),
    )
    asked = jnp.take(features, got_target.reshape(-1), axis=0).reshape(
        (owner_count, slot_depth) + features.shape[1:]
    )
    returned = lax.all_to_all(asked, "edge", split_axis=0, concat_axis=0, tiled=True)
    target_maps = jnp.take(
        returned.reshape((owner_count * slot_depth,) + features.shape[1:]), slot_index, axis=0
    )
    radius = WINDOW // 2
    source_maps = jnp.take(features, edge_source, axis=0)
    target_rows = padded_2(target_maps, (("tile", 1),), radius)
    target_padded = jnp.pad(target_rows, ((0, 0), (0, 0), (radius, radius), (0, 0)))
    columns = []
    for row_shift in range(WINDOW):
        for col_shift in range(WINDOW):
            moved = target_padded[
                :, row_shift : row_shift + band_rows, col_shift : col_shift + map_width
            ]
            columns.append(
                jnp.einsum("erwh,erwh->erw", source_maps, moved, preferred_element_type=jnp.float32)
            )
    corr = (jnp.stack(columns, axis=-1) * features.shape[3] ** (-0.5)).astype(jnp.bfloat16)
    motion = jax.nn.relu(
        jnp.einsum("ercd,dk->erck", corr, corr_weight, preferred_element_type=jnp.float32)
    ).astype(jnp.bfloat16)
    stacked = jnp.concatenate([hidden_state, motion], axis=-1)
    state_float = hidden_state.astype(jnp.float32)
    extended = padded_2(stacked, (("tile", 1),), 1)
    gates = jax.nn.sigmoid(convolve(pad_columns(extended), gate_weight))
    update = gates[..., :hidden_width]
    reset_state = (gates[..., hidden_width:] * state_float).astype(jnp.bfloat16)
    mixed = jnp.concatenate([reset_state, motion], axis=-1)
    mixed_extended = padded_2(mixed, (("tile", 1),), 1)
    candidate = jnp.tanh(convolve(pad_columns(mixed_extended), candidate_weight))
    new_state = ((1.0 - update) * state_float + update * candidate).astype(jnp.bfloat16)
    hidden_next = jnp.where(in_use[:, None, None, None], new_state, hidden_state)
    pixel_total = band_rows * map_width
    jacobian = jnp.einsum(
        "erwh,hk->ekrw", new_state, jacobian_weight, preferred_element_type=jnp.float32
    ).reshape(edge_total, 2, 12, pixel_total)
    confidence = jax.nn.softplus(
        jnp.einsum(
            "erwh,hk->ekrw", new_state, confidence_weight, preferred_element_type=jnp.float32
        )
    ).reshape(edge_total, 2, 1, pixel_total)
    normal_blocks = jnp.einsum(
        "ekap,ekbp->eab", jacobian * confidence, jacobian, precision=lax.Precision.HIGHEST
    ) / (MAPH * MAPW)
    normal_blocks = normal_blocks * in_use.astype(jnp.float32)[:, None, None]
    outgoing = jnp.concatenate(
        [
            normal_blocks[:, 6:, 6:].reshape(edge_total, 36),
            normal_blocks[:, :6, 6:].reshape(edge_total, 36),
        ],
        axis=1,
    )
    slot_blocks = jnp.einsum(
        "es,eq->sq", slot_hits.astype(jnp.float32), outgoing, precision=lax.Precision.HIGHEST
    ).reshape(owner_count, slot_depth, 72)
    incoming = lax.all_to_all(slot_blocks, "edge", split_axis=0, concat_axis=0, tiled=True).reshape(
        owner_count * slot_depth, 72
    )
    flat_target = got_target.reshape(-1)
    flat_source = got_source.reshape(-1)
    row_frames = jnp.concatenate(
        [source_global, target_global, my_index * frame_total + flat_target, flat_source]
    )
    col_frames = jnp.concatenate([edge_source, edge_source, flat_target, flat_target])
    block_list = jnp.concatenate(
        [
            normal_blocks[:, :6, :6],
            normal_blocks[:, 6:, :6],
            incoming[:, :36].reshape(-1, 6, 6),
            incoming[:, 36:].reshape(-1, 6, 6),
        ],
        axis=0,
    )
    on_diagonal = (row_frames == my_index * frame_total + col_frames).astype(jnp.float32)
    col_hits = (col_frames[:, None] == jnp.arange(frame_total)[None, :]).astype(jnp.float32)
    diagonal_part = jnp.einsum(
        "if,iq->fq",
        col_hits * on_diagonal[:, None],
        block_list.reshape(-1, 36),
        precision=lax.Precision.HIGHEST,
    )
    apart_blocks = block_list * (1.0 - on_diagonal)[:, None, None]
    spread = (apart_blocks[:, :, None, :] * col_hits[:, None, :, None]).reshape(
        -1, 6, frame_total * 6
    )
    own_rows = frame_total * owner_count * 6 // lax.axis_size("tile")
    frame_span = own_rows * lax.axis_size("tile") // 6
    row_hits = (row_frames[:, None] == jnp.arange(frame_span)[None, :]).astype(jnp.float32)
    placed = jnp.einsum("ic,ixq->cxq", row_hits, spread, precision=lax.Precision.HIGHEST)
    camera_hessian = lax.psum_scatter(
        placed.reshape(own_rows * lax.axis_size("tile"), frame_total * 6).astype(jnp.bfloat16),
        "tile",
        scatter_dimension=0,
        tiled=True,
    ).astype(jnp.float32)
    pose_diagonal = lax.psum(diagonal_part, "tile")
    return (hidden_next, camera_hessian, pose_diagonal)


def solution(mesh):
    placed = (
        P("edge", "tile", None, None),
        P("edge", "tile", None, None),
        P("edge"),
        P("edge", None),
        P("edge"),
        P("edge"),
        P(),
        P(),
        P(),
        P(),
        P(),
    )
    return jax.shard_map(
        per_device,
        mesh=mesh,
        in_specs=placed,
        out_specs=(P("edge", "tile", None, None), P("tile", "edge"), P("edge", None)),
        check_vma=False,
    )
```

profile of v0, /device:TPU:0, one launch (start us, length us, event | category | flops | bytes accessed | tf_op | source)
XLA Modules:
  0.0 204.7 jit_solution(6177645534464706526)
XLA Ops:
  11.0 9.7 %all_to_all.28 = s32[4,1,4]{2,1,0:T(1,128)S(1)} all-to-all(s32[4,1,4]{2,1,0:T(1,128)S(1)} %bitcast.304), channel_id=1, replica_groups=mesh['edge'=4,'tile'=8] {'edge'}, dimensions={0} | all-to-all | bytes 128 | tf_op jit(solution)/shard_map/all_to_all | solution.py:85
  22.0 1.9 gather_fusion.1
  23.9 2.8 %broadcast_select_fusion = bf16[4,4,6,64,128]{4,3,2,1,0:T(8,128)(2,1)} fusion(bf16[4,4,6,64,128]{4,3,2,1,0:T(8,128)(2,1)} %bitcast.251, pred[4,4]{1,0:T(4,128)(4,1)S(1)} %compare_and_fusion), kind=kLoop, calls=%fused_computation.176 | loop fusion | flops 786432 | bytes 3145744 | tf_op jit(solution)/shard_map/jit(_take)/select_n | solution.py:88
  26.6 4.3 %all-to-all-start.1 = ((bf16[4,4,6,64,128]{4,3,2,1,0:T(8,128)(2,1)}), bf16[4,4,6,64,128]{4,3,2,1,0:T(8,128)(2,1)}, u32[]{:S(2)}, u32[]{:S(2)}) async-start(bf16[4,4,6,64,128]{4,3,2,1,0:T(8,128)(2,1)} %broadcast_select_fusion), calls=%async_computation.1 | async-start | bytes 3145728 | tf_op jit(solution)/shard_map/all_to_all | solution.py:91
  33.7 15.4 %all-to-all-done.1 = bf16[4,4,6,64,128]{4,3,2,1,0:T(8,128)(2,1)} async-done(((bf16[4,4,6,64,128]{4,3,2,1,0:T(8,128)(2,1)}), bf16[4,4,6,64,128]{4,3,2,1,0:T(8,128)(2,1)}, u32[]{:S(2)}, u32[]{:S(2)}) %all-to-all-start.1) | async-done | bytes 1572896 | tf_op jit(solution)/shard_map/all_to_all | solution.py:91
  49.1 3.2 %all-to-all-start.2 = ((s32[4,1,4]{2,1,0:T(1,128)}), s32[4,1,4]{2,1,0:T(1,128)S(1)}, u32[]{:S(2)}, u32[]{:S(2)}) async-start(s32[4,1,4]{2,1,0:T(1,128)} %bitcast.116), calls=%async_computation.2 | async-start | bytes 4096 | tf_op jit(solution)/shard_map/all_to_all | solution.py:86
  52.4 2.1 %gather_fusion.2 = bf16[8,6,64,128]{3,2,1,0:T(8,128)(2,1)S(1)} fusion(bf16[16,6,64,128]{3,2,1,0:T(8,128)(2,1)} %bitcast.9, s32[1024]{0:T(1024)S(1)} %pad_clamp_fusion), kind=kCustom, calls=%fused_computation.2 | custom fusion | bytes 1572896 | tf_op jit(solution)/shard_map/jit(_take)/gather | solution.py:92
  54.7 1.3 collective-permute-start
  56.0 1.3 collective-permute-start.1
  59.3 2.1 %collective-permute-done.1 = bf16[8,3,64,128]{3,2,1,0:T(8,128)(2,1)S(1)} collective-permute-done((bf16[8,3,64,128]{3,2,1,0:T(8,128)(2,1)S(1)}, bf16[8,3,64,128]{3,2,1,0:T(8,128)(2,1)S(1)}, u32[]{:S(2)}, u32[]{:S(2)}) %collective-permute-start.1) | collective-permute-done | bytes 393248 | tf_op jit(solution)/shard_map/ppermute | solution.py:21
  62.4 7.7 %fusion.75 = (f32[8,6,64]{2,1,0:T(8,128)S(1)}, f32[8,6,64]{2,1,0:T(8,128)S(1)}, f32[8,6,64]{2,1,0:T(8,128)S(1)}, f32[8,6,64]{2,1,0:T(8,128)S(1)}, f32[8,6,64]{2,...) fusion(bf16[8,12,70,128]{3,2,1,0:T(8,128)(2,1)S(1)} %fusion.29,, ...), kind=kLoop, calls=%fused_computation.154 | loop fusion | flops 20788224 | bytes 14364680
  70.1 7.6 %fusion.95 = (f32[8,6,64]{2,1,0:T(8,128)S(1)}, f32[8,6,64]{2,1,0:T(8,128)S(1)}, f32[8,6,64]{2,1,0:T(8,128)S(1)}, f32[8,6,64]{2,1,0:T(8,128)S(1)}, f32[8,6,64]{2,...) fusion(bf16[8,12,70,128]{3,2,1,0:T(8,128)(2,1)S(1)} %fusion.29,, ...), kind=kLoop, calls=%fused_computation.174 | loop fusion | flops 20788224 | bytes 14364680
  77.8 3.6 %fusion.55 = (f32[8,6,64]{2,1,0:T(8,128)S(1)}, f32[8,6,64]{2,1,0:T(8,128)S(1)}, f32[8,6,64]{2,1,0:T(8,128)S(1)}, f32[8,6,64]{2,1,0:T(8,128)S(1)}, f32[8,6,64]{2,...) fusion(bf16[8,12,70,128]{3,2,1,0:T(8,128)(2,1)S(1)} %fusion.29, ...), kind=kLoop, calls=%fused_computation.134 | loop fusion | flops 10199040 | bytes 7176200
  89.4 3.4 %fusion.92 = (f32[8,6,64]{2,1,0:T(8,128)S(1)}, f32[8,6,64]{2,1,0:T(8,128)S(1)}, f32[8,6,64]{2,1,0:T(8,128)S(1)}, f32[8,6,64]{2,1,0:T(8,128)S(1)}, f32[8,6,64]{2,...) fusion(bf16[8,3,64,128]{3,2,1,0:T(8,128)(2,1)S(1)} %collective-permute-done.1, ...), kind=kLoop, calls=%fused_computation.171 | loop fusion | flops 11381760 | bytes 2445320
  93.0 8.1 %stack.199 = f32[8,6,64,49]{2,3,1,0:T(8,128)} concatenate(f32[8,6,64,1]{2,3,1,0:T(1,128)} %copy.199, f32[8,6,64,1]{2,3,1,0:T(1,128)} %copy.200, f32[8,6,64,1]{2,3,1,0:T(1,128)} %copy.201, f32[8,6,64,1]{2,3,1,0:T(1,128)S(1)} %copy.202, f32[8,6,64,1]{2,3,1,0:T(1,128)} %copy.203, f32[8,6,64,1]{2,3,1,0:T(1,128)} %copy.204, f32[8,6,64,1]{2,3,1,0:T(1,128)} %copy.205, ...), dimensions={3} | concatenate | bytes 1204224 | tf_op jit(solution)/shard_map/stack | solution.py:108
  101.1 1.8 maximum_convert_fusion
  103.1 8.0 %collective-permute-start.2 = (bf16[8,1,64,256]{3,2,1,0:T(8,128)(2,1)S(1)}, bf16[8,1,64,256]{3,2,1,0:T(8,128)(2,1)S(1)}, u32[]{:S(2)}, u32[]{:S(2)}) collective-permute-start(bf16[8,1,64,256]{3,2,1,0:T(8,128)(2,1)S(1)} %get-tuple-element.63), channel_id=1, source_target_pairs={{0,1},{1,2},{2,3},{3,4},{4,5},{5,6},{6,7},{8,9},{9,10},{10,11},{11... | collective-permute-start | bytes 786440 | tf_op jit(solution)/shard_map/ppermute | solution.py:19
  113.0 1.5 collective-permute-done.3
  117.8 2.2 %fusion.15 = f32[8,6,64,256]{3,2,1,0:T(8,128)} fusion(bf16[8,6,64,128]{3,2,1,0:T(8,128)(2,1)S(1)} %maximum_convert_fusion, bf16[8,6,64,128]{3,2,1,0:T(8,128)(2,1)S(1)} %copy-done.2, bf16[8,1,64,256]{3,2,1,0:T(8,128)(2,1)S(1)} %collective-permute-done.2, bf16[3,3,256,256]{3,2,1,0:T(8,128)(2,1)S(1)} %copy-done.4), kind=kOutput, calls=%fused_computation.84 | convolution fusion | flops 408158208 | bytes 5111808 | tf_op jit(solution)/shard_map/erwc,ck->erwk/dot_general | solution.py:39
  120.0 2.3 %fusion.9 = f32[8,6,64,256]{3,2,1,0:T(8,128)} fusion(bf16[8,6,64,128]{3,2,1,0:T(8,128)(2,1)S(1)} %maximum_convert_fusion, bf16[8,1,64,256]{3,2,1,0:T(8,128)(2,1)S(1)} %collective-permute-done.3, bf16[8,6,64,128]{3,2,1,0:T(8,128)(2,1)S(1)} %copy-done.2, bf16[3,3,256,256]{3,2,1,0:T(8,128)(2,1)S(1)} %copy-done.4), kind=kOutput, calls=%fused_computation.80 | convolution fusion | flops 408158208 | bytes 5111808 | tf_op jit(solution)/shard_map/erwc,ck->erwk/dot_general | solution.py:39
  122.3 5.2 %add_divide_fusion = f32[8,6,64,256]{3,2,1,0:T(8,128)} fusion(f32[8,6,64,256]{3,2,1,0:T(8,128)} %fusion.9, f32[8,6,64,256]{3,2,1,0:T(8,128)S(1)} %fusion.34, f32[8,6,64,256]{3,2,1,0:T(8,128)S(1)} %fusion.33, f32[8,6,64,256]{3,2,1,0:T(8,128)S(1)} %fusion.45, f32[8,6,64,256]{3,2,1,0:T(8,128)S(1)} %fusion.32, f32[8,6,64,256]{3,2,1,0:T(8,128)S(1)} %fusion.31, ...), kind=kOutput, calls=%fused_computation.55 | convolution fusion | flops 411303936 | bytes 30539776 | tf_op jit(solution)/shard_map/erwc,ck->erwk/dot_general | solution.py:39
  127.5 1.7 fusion.44
  129.3 6.3 %collective-permute-start.4 = (bf16[8,1,64,256]{3,2,1,0:T(8,128)(2,1)S(1)}, bf16[8,1,64,256]{3,2,1,0:T(8,128)(2,1)S(1)}, u32[]{:S(2)}, u32[]{:S(2)}) collective-permute-start(bf16[8,1,64,256]{3,2,1,0:T(8,128)(2,1)S(1)} %get-tuple-element.61), channel_id=1, source_target_pairs={{0,1},{1,2},{2,3},{3,4},{4,5},{5,6},{6,7},{8,9},{9,10},{10,11},{11... | collective-permute-start | bytes 786440 | tf_op jit(solution)/shard_map/ppermute | solution.py:19
  135.6 1.5 collective-permute-start.5
  137.7 1.3 collective-permute-done.5
  143.4 1.3 copy-done.3
  144.7 2.3 %broadcast_select_fusion.3 = (bf16[8,6,64,128]{3,2,1,0:T(8,128)(2,1)}, bf16[8,6,64,128]{3,2,1,0:T(8,128)(2,1)S(1)}) fusion(bf16[8,6,64,128]{3,2,1,0:T(8,128)(2,1)S(1)} %copy-done.2, pred[8]{0:T(512)(128)(4,1)S(1)} %copy-done.15, bf16[3,3,256,128]{3,2,1,0:T(8,128)(2,1)S(1)} %copy-done.5, bf16[8,8,64,256]{3,2,1,0:T(8,128)(2,1)S(1)} %fusion.4, ...), kind=kOutput, calls=%fused_computation.199 | convolution fusion | flops 207224832 | bytes 18678272 | tf_op jit(solution)/shard_map/erwc,ck->erwk/dot_general | solution.py:39
  151.0 4.2 %all-to-all-start.3 = ((f32[4,4,72]{2,1,0:T(4,128)}), f32[4,4,72]{2,1,0:T(4,128)S(1)}, u32[]{:S(2)}, u32[]{:S(2)}) async-start(f32[4,4,72]{2,1,0:T(4,128)} %bitcast.126), calls=%async_computation.3 | async-start | bytes 16384 | tf_op jit(solution)/shard_map/all_to_all | solution.py:146
  155.5 4.4 %all-to-all-done.3 = f32[4,4,72]{2,1,0:T(4,128)S(1)} async-done(((f32[4,4,72]{2,1,0:T(4,128)}), f32[4,4,72]{2,1,0:T(4,128)S(1)}, u32[]{:S(2)}, u32[]{:S(2)}) %all-to-all-start.3) | async-done | bytes 4640 | tf_op jit(solution)/shard_map/all_to_all | solution.py:146
  163.9 28.7 %psum.7 = f32[24,36]{1,0:T(8,128)} all-reduce(f32[24,36]{1,0:T(8,128)S(1)} %fusion.148), channel_id=1, replica_groups=mesh['edge'=4,'tile'=8] {'tile'}, use_global_device_ids=true, to_apply=%region_5.6 | all-reduce | flops 864 | bytes 6912 | tf_op jit(solution)/shard_map/psum | solution.py:186
  192.6 3.9 %reduce-scatter.2.cloned.1.call-done = bf16[72,144]{1,0:T(8,128)(2,1)} async-done(((bf16[576,144]{1,0:T(8,128)(2,1)}), bf16[72,144]{1,0:T(8,128)(2,1)}) %reduce-scatter.2.cloned.1.call-update) | async-done | bytes 20752 | tf_op jit(solution)/shard_map/reduce_scatter | solution.py:180
  196.5 1.4 convert_element_type.74
  (174 shorter events, 36.5 us)
Async XLA Ops:
  7.2 14.8 %copy-start = (bf16[24,6,64,128]{3,2,1,0:T(8,128)(2,1)S(1)}, bf16[24,6,64,128]{3,2,1,0:T(8,128)(2,1)}, u32[]{:S(2)}) copy-start(bf16[24,6,64,128]{3,2,1,0:T(8,128)(2,1)} %param.11) | copy-start | bytes 7077892
  26.6 22.5 %all-to-all-start.1 = ((bf16[4,4,6,64,128]{4,3,2,1,0:T(8,128)(2,1)}), bf16[4,4,6,64,128]{4,3,2,1,0:T(8,128)(2,1)}, u32[]{:S(2)}, u32[]{:S(2)}) async-start(bf16[4,4,6,64,128]{4,3,2,1,0:T(8,128)(2,1)} %broadcast_select_fusion), calls=%async_computation.1 | async-start | bytes 3145728 | tf_op jit(solution)/shard_map/all_to_all | solution.py:91
  31.0 2.7 %copy-start.14 = (s32[8]{0:T(128)S(1)}, s32[8]{0:T(128)}, u32[]{:S(2)}) copy-start(s32[8]{0:T(128)} %param.13) | copy-start | bytes 100
  31.0 2.7 %copy-start.11 = (s32[8,1]{0,1:T(1,128)S(1)}, s32[8,1]{0,1:T(1,128)}, u32[]{:S(2)}) copy-start(s32[8,1]{0,1:T(1,128)} %param.14) | copy-start | bytes 100
  31.0 2.7 %copy-start.17 = (s32[8]{0:T(128)S(1)}, s32[8]{0:T(128)}, u32[]{:S(2)}) copy-start(s32[8]{0:T(128)} %param.15) | copy-start | bytes 100
  49.1 8.8 %all-to-all-start.2 = ((s32[4,1,4]{2,1,0:T(1,128)}), s32[4,1,4]{2,1,0:T(1,128)S(1)}, u32[]{:S(2)}, u32[]{:S(2)}) async-start(s32[4,1,4]{2,1,0:T(1,128)} %bitcast.116), calls=%async_computation.2 | async-start | bytes 4096 | tf_op jit(solution)/shard_map/all_to_all | solution.py:86
  54.7 4.6 %collective-permute-start = (bf16[8,3,64,128]{3,2,1,0:T(8,128)(2,1)S(1)}, bf16[8,3,64,128]{3,2,1,0:T(8,128)(2,1)S(1)}, u32[]{:S(2)}, u32[]{:S(2)}) collective-permute-start(bf16[8,3,64,128]{3,2,1,0:T(8,128)(2,1)S(1)} %get-tuple-element.65), channel_id=1, source_target_pairs={{0,1},{1,2},{2,3},{3,4},{4,5},{5,6},{6,7},{8,9},{9,10},{10,11},{11... | collective-permute-start | bytes 1179656 | tf_op jit(solution)/shard_map/ppermute | solution.py:19
  56.0 5.4 %collective-permute-start.1 = (bf16[8,3,64,128]{3,2,1,0:T(8,128)(2,1)S(1)}, bf16[8,3,64,128]{3,2,1,0:T(8,128)(2,1)S(1)}, u32[]{:S(2)}, u32[]{:S(2)}) collective-permute-start(bf16[8,3,64,128]{3,2,1,0:T(8,128)(2,1)S(1)} %get-tuple-element.66), channel_id=1, source_target_pairs={{1,0},{2,1},{3,2},{4,3},{5,4},{6,5},{7,6},{9,8},{10,9},{11,10},{12... | collective-permute-start | bytes 1179656 | tf_op jit(solution)/shard_map/ppermute | solution.py:21
  88.1 4.9 %copy-start.6 = (f32[8,6,64,1]{2,3,1,0:T(1,128)S(1)}, f32[8,6,64,1]{2,3,1,0:T(1,128)}, u32[]{:S(2)}) copy-start(f32[8,6,64,1]{2,3,1,0:T(1,128)} %copy.227) | copy-start | bytes 36868
  88.1 4.9 %copy-start.7 = (f32[8,6,64,1]{2,3,1,0:T(1,128)S(1)}, f32[8,6,64,1]{2,3,1,0:T(1,128)}, u32[]{:S(2)}) copy-start(f32[8,6,64,1]{2,3,1,0:T(1,128)} %copy.228) | copy-start | bytes 36868
  88.1 4.9 %copy-start.8 = (f32[8,6,64,1]{2,3,1,0:T(1,128)S(1)}, f32[8,6,64,1]{2,3,1,0:T(1,128)}, u32[]{:S(2)}) copy-start(f32[8,6,64,1]{2,3,1,0:T(1,128)} %copy.229) | copy-start | bytes 36868
  92.7 8.4 %copy-start.9 = (bf16[49,128]{1,0:T(8,128)(2,1)S(1)}, bf16[49,128]{1,0:T(8,128)(2,1)}, u32[]{:S(2)}) copy-start(bf16[49,128]{1,0:T(8,128)(2,1)} %param.17) | copy-start | bytes 37636
  101.1 1.8 copy-start.2
  103.0 9.4 %copy-start.4 = (bf16[3,3,256,256]{3,2,1,0:T(8,128)(2,1)S(1)}, bf16[3,3,256,256]{3,2,1,0:T(8,128)(2,1)}, u32[]{:S(2)}) copy-start(bf16[3,3,256,256]{3,2,1,0:T(8,128)(2,1)} %param.18) | copy-start | bytes 3538948
  103.1 9.9 %collective-permute-start.2 = (bf16[8,1,64,256]{3,2,1,0:T(8,128)(2,1)S(1)}, bf16[8,1,64,256]{3,2,1,0:T(8,128)(2,1)S(1)}, u32[]{:S(2)}, u32[]{:S(2)}) collective-permute-start(bf16[8,1,64,256]{3,2,1,0:T(8,128)(2,1)S(1)} %get-tuple-element.63), channel_id=1, source_target_pairs={{0,1},{1,2},{2,3},{3,4},{4,5},{5,6},{6,7},{8,9},{9,10},{10,11},{11... | collective-permute-start | bytes 786440 | tf_op jit(solution)/shard_map/ppermute | solution.py:19
  111.1 3.4 %collective-permute-start.3 = (bf16[8,1,64,256]{3,2,1,0:T(8,128)(2,1)S(1)}, bf16[8,1,64,256]{3,2,1,0:T(8,128)(2,1)S(1)}, u32[]{:S(2)}, u32[]{:S(2)}) collective-permute-start(bf16[8,1,64,256]{3,2,1,0:T(8,128)(2,1)S(1)} %get-tuple-element.64), channel_id=1, source_target_pairs={{1,0},{2,1},{3,2},{4,3},{5,4},{6,5},{7,6},{9,8},{10,9},{11,10},{12... | collective-permute-start | bytes 786440 | tf_op jit(solution)/shard_map/ppermute | solution.py:21
  129.2 7.9 %copy-start.5 = (bf16[3,3,256,128]{3,2,1,0:T(8,128)(2,1)S(1)}, bf16[3,3,256,128]{3,2,1,0:T(8,128)(2,1)}, u32[]{:S(2)}) copy-start(bf16[3,3,256,128]{3,2,1,0:T(8,128)(2,1)} %param.19) | copy-start | bytes 1769476
  129.3 8.4 %collective-permute-start.4 = (bf16[8,1,64,256]{3,2,1,0:T(8,128)(2,1)S(1)}, bf16[8,1,64,256]{3,2,1,0:T(8,128)(2,1)S(1)}, u32[]{:S(2)}, u32[]{:S(2)}) collective-permute-start(bf16[8,1,64,256]{3,2,1,0:T(8,128)(2,1)S(1)} %get-tuple-element.61), channel_id=1, source_target_pairs={{0,1},{1,2},{2,3},{3,4},{4,5},{5,6},{6,7},{8,9},{9,10},{10,11},{11... | collective-permute-start | bytes 786440 | tf_op jit(solution)/shard_map/ppermute | solution.py:19
  135.6 3.4 %collective-permute-start.5 = (bf16[8,1,64,256]{3,2,1,0:T(8,128)(2,1)S(1)}, bf16[8,1,64,256]{3,2,1,0:T(8,128)(2,1)S(1)}, u32[]{:S(2)}, u32[]{:S(2)}) collective-permute-start(bf16[8,1,64,256]{3,2,1,0:T(8,128)(2,1)S(1)} %get-tuple-element.62), channel_id=1, source_target_pairs={{1,0},{2,1},{3,2},{4,3},{5,4},{6,5},{7,6},{9,8},{10,9},{11,10},{12... | collective-permute-start | bytes 786440 | tf_op jit(solution)/shard_map/ppermute | solution.py:21
  142.8 1.9 copy-start.3
  142.8 1.9 copy-start.15
  144.7 2.3 %copy-start.10 = (bf16[128,24]{0,1:T(8,128)(2,1)S(1)}, bf16[128,24]{0,1:T(8,128)(2,1)}, u32[]{:S(2)}) copy-start(bf16[128,24]{0,1:T(8,128)(2,1)} %param.20) | copy-start | bytes 18436
  147.7 0.7 copy-start.19
  147.9 1.4 copy-start.16
  148.4 6.8 %copy-start.12 = (s32[48]{0:T(128)S(1)}, s32[48]{0:T(128)}, u32[]{:S(2)}) copy-start(s32[48]{0:T(128)} %get-tuple-element.59) | copy-start | bytes 580
  151.0 8.9 %all-to-all-start.3 = ((f32[4,4,72]{2,1,0:T(4,128)}), f32[4,4,72]{2,1,0:T(4,128)S(1)}, u32[]{:S(2)}, u32[]{:S(2)}) async-start(f32[4,4,72]{2,1,0:T(4,128)} %bitcast.126), calls=%async_computation.3 | async-start | bytes 16384 | tf_op jit(solution)/shard_map/all_to_all | solution.py:146
  155.2 41.3 %reduce-scatter.2.cloned.1.call-start = ((), (), s32[]{:S(2)}) async-start(), calls=%async_computation.5 | async-start | bytes 331776 | tf_op jit(solution)/shard_map/reduce_scatter | solution.py:180
  160.2 37.7 %copy-start.1 = (bf16[24,6,64,128]{3,2,1,0:T(8,128)(2,1)S(1)}, bf16[24,6,64,128]{3,2,1,0:T(8,128)(2,1)}, u32[]{:S(2)}) copy-start(bf16[24,6,64,128]{3,2,1,0:T(8,128)(2,1)} %param.11) | copy-start | bytes 7077892
  160.3 3.5 %copy-start.13 = (s32[48]{0:T(128)S(1)}, s32[48]{0:T(128)}, u32[]{:S(2)}) copy-start(s32[48]{0:T(128)} %get-tuple-element.59) | copy-start | bytes 580
  160.4 3.4 %copy-start.18 = (f32[48]{0:T(128)S(1)}, f32[48]{0:T(128)}, u32[]{:S(2)}) copy-start(f32[48]{0:T(128)} %get-tuple-element.58) | copy-start | bytes 580
Sparse Core Ops, SparseCore 0:
  163.7 32.7 reduce-scatter.1
where the time goes:
time: 206 us; the launch traced here: 205 us
  blocking collectives  38.4 us (19%)
  other arithmetic  36.9 us (18%)
  starting transfers between devices  31.5 us (15%)
  waiting for transfers between devices  28.7 us (14%)
  local copies, waits for them, and re-layouts  27.6 us (13%)
  matrix products  26.1 us (13%)
  between operations  15.6 us (8%)
    psum x1, blocking collectives, per_device(): pose_diagonal = lax.psum(diagonal_part, 'tile')  28.7 us
    unnamed x4, other arithmetic  22.3 us
    dot_general x18, matrix products, convolve(): jnp.einsum('erwc,ck->erwk', window, weight[row_step, col_step], preferred...  20.2 us
    another operation x50, local copies, waits for them, and re-layouts, per_device(): jnp.stack(columns, axis=-1) * features.shape[3] ** (-0.5)  16 us
    ppermute x3, starting transfers between devices, padded_2(): lax.ppermute(tail, axis, [(i, (i + 1) % count) for i in range(ends)])  15.7 us
    all_to_all x1, waiting for transfers between devices, per_device(): lax.all_to_all(asked, 'edge', split_axis=0, concat_axis=0, tiled=True)  15.4 us
    all_to_all x1, blocking collectives, per_device(): lax.all_to_all(send_target, 'edge', split_axis=0, concat_axis=0, tiled=True)  9.66 us
    ppermute x3, waiting for transfers between devices, padded_2(): lax.ppermute(head, axis, [((i + 1) % count, i) for i in range(ends)])  4.95 us
  transfers between devices with their start and end apart: 10, of which 6 were waited for; matrix products, arithmetic and copies ran while one was open for 4% of the time, Pallas kernels for 0%

commit v1 on v0

v1 whole, which is shorter than its diff:
```python
import functools

import jax
import jax.numpy as jnp
from jax import lax
from jax.experimental import pallas as pl
from jax.experimental.pallas import tpu as pltpu
from jax.sharding import PartitionSpec as P

MAPH = 48
WINDOW = 7
RADIUS = WINDOW // 2
MESH = pl.DeviceIdType.MESH
HIGH = lax.Precision.HIGHEST
BF = jnp.bfloat16
F32 = jnp.float32


def nt(a, b, precision=None):
    return lax.dot_general(
        a, b, (((1,), (1,)), ((), ())), preferred_element_type=F32, precision=precision
    )


def nn(a, b, precision=None):
    return lax.dot_general(
        a, b, (((1,), (0,)), ((), ())), preferred_element_type=F32, precision=precision
    )


def iota(shape, dim):
    return lax.broadcasted_iota(jnp.int32, shape, dim)


def sixth(index):
    return jnp.floor((index.astype(F32) + 0.5) * (1.0 / 6.0))


def kernel(
    dims,
    meta_in,
    feat,
    hidden,
    corr_w,
    gate_w,
    cand_w,
    head_w,
    out_hidden,
    out_cam,
    out_diag,
    meta_all,
    meta_s,
    send,
    text,
    sref,
    hext,
    mext,
    rext,
    x3,
    wh,
    wm,
    wr,
    gpre,
    cpre,
    upd,
    gpart,
    gtile,
    gsum,
    gall,
    s_meta,
    r_meta,
    l_meta,
    s_feat,
    r_feat,
    s_tup,
    r_tup,
    s_tdn,
    r_tdn,
    s_hup,
    r_hup,
    s_hdn,
    r_hdn,
    s_mup,
    r_mup,
    s_mdn,
    r_mdn,
    s_rup,
    r_rup,
    s_rdn,
    r_rdn,
    s_gt,
    r_gt,
    s_ge,
    r_ge,
):
    n_edge, n_tile, edges, frames, rows, width, slots = dims
    band = rows * width
    halo = RADIUS * width
    me = lax.axis_index("edge")
    tile = lax.axis_index("tile")
    up, down = tile - 1, tile + 1
    has_up, has_down = tile > 0, tile < n_tile - 1

    barrier = pltpu.get_barrier_semaphore()
    for rel in range(1, n_edge):
        pl.semaphore_signal(
            barrier, inc=1, device_id=((me + rel) % n_edge, tile), device_id_type=MESH
        )
    for rel in range(1, n_tile):
        pl.semaphore_signal(
            barrier, inc=1, device_id=(me, (tile + rel) % n_tile), device_id_type=MESH
        )
    pl.semaphore_wait(barrier, n_edge + n_tile - 2)

    def remote(src, dst, send_sem, recv_sem, edge_id, tile_id):
        return pltpu.make_async_remote_copy(
            src_ref=src,
            dst_ref=dst,
            send_sem=send_sem,
            recv_sem=recv_sem,
            device_id=(edge_id, tile_id),
            device_id_type=MESH,
        )

    def meta_copy(rel):
        return remote(
            meta_in, meta_all.at[me], s_meta.at[rel], r_meta.at[rel], (me + rel) % n_edge, tile
        )

    for rel in range(1, n_edge):
        meta_copy(rel).start()

    def hid_up(e):
        return remote(
            hidden.at[e, pl.ds(0, width)], hext.at[e, pl.ds(width + band, width)],
            s_hup.at[e], r_hup.at[e], me, up,
        )

    def hid_dn(e):
        return remote(
            hidden.at[e, pl.ds(band - width, width)], hext.at[e, pl.ds(0, width)],
            s_hdn.at[e], r_hdn.at[e], me, down,
        )

    def row_up(buf, s, r, e):
        return remote(
            buf.at[e, pl.ds(width, width)], buf.at[e, pl.ds(width + band, width)],
            s.at[e], r.at[e], me, up,
        )

    def row_dn(buf, s, r, e):
        return remote(
            buf.at[e, pl.ds(band, width)], buf.at[e, pl.ds(0, width)],
            s.at[e], r.at[e], me, down,
        )

    def txt_up(k):
        return remote(
            text.at[k, pl.ds(halo, halo)], text.at[k, pl.ds(halo + band, halo)],
            s_tup.at[k], r_tup.at[k], me, up,
        )

    def txt_dn(k):
        return remote(
            text.at[k, pl.ds(band, halo)], text.at[k, pl.ds(0, halo)],
            s_tdn.at[k], r_tdn.at[k], me, down,
        )

    def start_pair(make_up, make_dn):
        @pl.when(has_up)
        def _():
            make_up.start()

        @pl.when(has_down)
        def _():
            make_dn.start()

    def recv_pair(make_up, make_dn):
        @pl.when(has_down)
        def _():
            make_up.wait_recv()

        @pl.when(has_up)
        def _():
            make_dn.wait_recv()

    def sent_pair(make_up, make_dn):
        @pl.when(has_up)
        def _():
            make_up.wait_send()

        @pl.when(has_down)
        def _():
            make_dn.wait_send()

    def each(count, body):
        def step(i, carry):
            body(i)
            return carry

        lax.fori_loop(0, count, step, 0)

    each(edges, lambda e: start_pair(hid_up(e), hid_dn(e)))

    zero_row = jnp.zeros((width, 128), BF)
    zero_halo = jnp.zeros((halo, 128), BF)

    @pl.when(tile == 0)
    def _():
        def clear(e):
            for buf in (hext, mext, rext):
                buf[e, pl.ds(0, width)] = zero_row

        each(edges, clear)

        def clear_text(k):
            text[k, pl.ds(0, halo)] = zero_halo

        each(n_edge * slots, clear_text)

    @pl.when(tile == n_tile - 1)
    def _():
        def clear(e):
            for buf in (hext, mext, rext):
                buf[e, pl.ds(width + band, width)] = zero_row

        each(edges, clear)

        def clear_text(k):
            text[k, pl.ds(halo + band, halo)] = zero_halo

        each(n_edge * slots, clear_text)

    if (rows + 2 * RADIUS) % 2:

        def clear_pad(k):
            text[k, pl.ds(band + 2 * halo, width)] = zero_row

        each(n_edge * slots, clear_pad)

    meta_all[me] = meta_in[...]
    for rel in range(1, n_edge):
        remote(
            meta_in, meta_all.at[(me - rel + n_edge) % n_edge], s_meta.at[rel], r_meta.at[rel],
            (me + rel) % n_edge, tile,
        ).wait_recv()
    local = pltpu.make_async_copy(meta_all, meta_s, l_meta)
    local.start()
    local.wait()

    def asked(peer):
        picks = [jnp.int32(0)] * slots
        rank = jnp.int32(0)
        for k in range(edges):
            hit = (meta_s[peer, 0, k] == me).astype(jnp.int32)
            goal = meta_s[peer, 0, 8 + k]
            for s in range(slots):
                picks[s] = jnp.where((hit == 1) & (rank == s), goal, picks[s])
            rank = rank + hit
        return picks

    def feat_copy(rel, s):
        return remote(
            send.at[(rel - 1) * slots + s],
            text.at[rel * slots + s, pl.ds(halo, band)],
            s_feat.at[rel * slots + s],
            r_feat.at[rel * slots + s],
            (me - rel + n_edge) % n_edge,
            tile,
        )

    asks = [asked((me - rel + n_edge) % n_edge) for rel in range(n_edge)]
    for s in range(slots):
        for rel in range(1, n_edge):
            send[(rel - 1) * slots + s] = feat[asks[rel][s]]
        for rel in range(1, n_edge):
            feat_copy(rel, s).start()
    for s in range(slots):
        text[s, pl.ds(halo, band)] = feat[asks[0][s]]
    for s in range(slots):
        start_pair(txt_up(s), txt_dn(s))

    for a in range(3):
        for b in range(3):
            at = pl.ds((a * 3 + b) * 128, 128)
            wh[at, :] = gate_w[a, b, 0:128, :]
            wm[at, 0:256] = gate_w[a, b, 128:256, :]
            wm[at, 256:384] = cand_w[a, b, 128:256, :]
            wr[at, :] = cand_w[a, b, 0:128, :]

    col = iota((band + 2 * width, 128), 0) & (width - 1)

    def shifted(buf, e):
        value = buf[e]
        wide = value.astype(F32)
        left = jnp.where(col == 0, 0.0, pltpu.roll(wide, 1, 0)).astype(BF)
        right = jnp.where(
            col == width - 1, 0.0, pltpu.roll(wide, band + 2 * width - 1, 0)
        ).astype(BF)
        x3[:, 0:128] = left
        x3[:, 128:256] = value
        x3[:, 256:384] = right
        return jnp.concatenate(
            [x3[0:band], x3[width : width + band], x3[2 * width : 2 * width + band]], axis=1
        )

    flip_row, flip_col = iota((2 * width, 2 * width), 0), iota((2 * width, 2 * width), 1)
    flip = (
        ((flip_row >= width) == (flip_col >= width))
        & ((flip_row & (width - 1)) + (flip_col & (width - 1)) == width - 1)
    ).astype(F32).astype(BF)

    def flipped(value):
        count = value.shape[0]
        return nn(flip[0:count, 0:count], value).astype(BF)

    def state_part(e):
        source = feat[meta_s[me, 0, 16 + e]]
        for first in range(0, rows, 2):
            last = min(rows, first + 2) * width
            sref[e, pl.ds(first * width, last - first * width)] = flipped(
                source[first * width : last]
            )
        hext[e, pl.ds(width, band)] = hidden[e]
        recv_pair(hid_up(e), hid_dn(e))
        gpre[e] = nn(shifted(hext, e), wh[...])

    each(edges, state_part)

    for s in range(slots):
        for rel in range(1, n_edge):
            feat_copy(rel, s).wait_recv()
            start_pair(txt_up(rel * slots + s), txt_dn(rel * slots + s))
    each(n_edge * slots, lambda k: recv_pair(txt_up(k), txt_dn(k)))

    lane = iota((width, 128), 1)
    place = (width - 1 - iota((width, 128), 0)) + ((lane + 97) & 63) - 32
    inside = (place >= 0) & (place < width)
    scale = 128.0 ** (-0.5)

    def slot_of(e):
        mine = meta_s[me, 0, e]
        rank = jnp.int32(0)
        for k in range(edges):
            rank = rank + jnp.where((meta_s[me, 0, k] == mine) & (k < e), 1, 0)
        return ((mine - me + n_edge) % n_edge) * slots + jnp.minimum(rank, slots - 1)

    def motion(e):
        k = slot_of(e)
        source = sref[e]
        target = text[k]
        for first in range(0, rows, 2):
            count = min(2, rows - first)
            table = nt(
                source[first * width : (first + count) * width],
                target[first * width : (first + 8) * width],
            )
            values = []
            for par in range(count):
                parts = []
                for g in range(4):
                    piece = table[par * width : (par + 1) * width, g * 128 : (g + 1) * 128]
                    moved = pltpu.roll(piece, 0, 1, stride=1, stride_axis=0)
                    parts.append(jnp.where(inside, moved * scale, 0.0).astype(BF))
                value = nn(jnp.concatenate(parts, axis=1), corr_w[par])
                values.append(jnp.maximum(value, 0.0).astype(BF))
            mext[e, pl.ds((first + 1) * width, count * width)] = flipped(
                jnp.concatenate(values, axis=0)
            )
        start_pair(row_up(mext, s_mup, r_mup, e), row_dn(mext, s_mdn, r_mdn, e))

    each(edges, motion)

    def gates(e):
        recv_pair(row_up(mext, s_mup, r_mup, e), row_dn(mext, s_mdn, r_mdn, e))
        both = nn(shifted(mext, e), wm[...])
        cpre[e] = both[:, 256:384]
        gate = jax.nn.sigmoid(gpre[e] + both[:, 0:256])
        upd[e] = gate[:, 0:128]
        rext[e, pl.ds(width, band)] = (gate[:, 128:256] * hidden[e].astype(F32)).astype(BF)
        start_pair(row_up(rext, s_rup, r_rup, e), row_dn(rext, s_rdn, r_rdn, e))

    each(edges, gates)

    gpart[...] = jnp.zeros_like(gpart)
    lane16 = iota((16, 128), 1)
    row16 = iota((16, 128), 0)

    def finish(e):
        recv_pair(row_up(rext, s_rup, r_rup, e), row_dn(rext, s_rdn, r_rdn, e))
        candidate = jnp.tanh(cpre[e] + nn(shifted(rext, e), wr[...]))
        update = upd[e]
        state = hidden[e]
        fresh = ((1.0 - update) * state.astype(F32) + update * candidate).astype(BF)
        used = (e < meta_s[me, 0, 24]).astype(F32)
        live = jnp.full((band, 128), used) > 0.5
        out_hidden[e] = jnp.where(live, fresh, state)
        heads = nn(fresh, head_w[...])
        jac = heads[:, 0:128]
        weighted = jac * jax.nn.softplus(heads[:, 128:256])
        square = lax.dot_general(
            weighted, jac, (((0,), (0,)), ((), ())), preferred_element_type=F32, precision=HIGH
        )
        other = pltpu.roll(pltpu.roll(square, 116, 0), 116, 1)
        block = (square + other)[0:16] * (used / (MAPH * width))
        block = jnp.where((lane16 < 12) & (row16 < 12), block, 0.0)
        gpart[...] += pltpu.roll(block, e * 16, 1)

    each(edges, finish)

    def tile_copy(rel):
        return remote(
            gpart, gtile.at[tile], s_gt.at[rel], r_gt.at[rel], me, (tile + rel) % n_tile
        )

    for rel in range(1, n_tile):
        tile_copy(rel).start()
    gtile[tile] = gpart[...]
    for rel in range(1, n_tile):
        remote(
            gpart, gtile.at[(tile - rel + n_tile) % n_tile], s_gt.at[rel], r_gt.at[rel],
            me, (tile + rel) % n_tile,
        ).wait_recv()
    total = gtile[0]
    for k in range(1, n_tile):
        total = total + gtile[k]
    gsum[...] = total

    def edge_copy(rel):
        return remote(gsum, gall.at[me], s_ge.at[rel], r_ge.at[rel], (me + rel) % n_edge, tile)

    for rel in range(1, n_edge):
        edge_copy(rel).start()
    gall[me] = total
    for rel in range(1, n_edge):
        remote(
            gsum, gall.at[(me - rel + n_edge) % n_edge], s_ge.at[rel], r_ge.at[rel],
            (me + rel) % n_edge, tile,
        ).wait_recv()

    cam_rows, cam_cols = out_cam.shape
    row_id = iota((cam_rows, 128), 0) + tile * cam_rows
    col_id = iota((cam_cols, 128), 0) + me * cam_cols
    same = (iota((128, 128), 0) >> 4) == (iota((128, 128), 1) >> 4)
    lefts, rights = [], []
    for j in range(n_edge):
        spots = meta_all[j, 1:2, :]
        mine = (col_id == spots).astype(F32)
        left = jnp.concatenate([(row_id == spots).astype(F32), mine], axis=0)
        stack = jnp.concatenate([gall[j]] * 8, axis=0)
        lefts.append(nn(left, jnp.where(same, stack, 0.0), HIGH))
        rights.append(mine)
    placed = nt(jnp.concatenate(lefts, axis=1), jnp.concatenate(rights, axis=1), HIGH)
    cam = placed[0:cam_rows]
    row_frame = sixth(iota((cam_rows, cam_cols), 0) + tile * cam_rows)
    col_frame = sixth(iota((cam_rows, cam_cols), 1) + me * cam_cols)
    out_cam[...] = jnp.where(row_frame == col_frame, 0.0, cam)
    own = placed[cam_rows:]
    own_row = sixth(iota((cam_cols, cam_cols), 0))
    own_col = sixth(iota((cam_cols, cam_cols), 1))
    own = jnp.where(own_row == own_col, own, 0.0)
    wide_row = iota((cam_cols, 128), 0)
    wide_lane = iota((cam_cols, 128), 1)
    row_in = wide_row.astype(F32) - 6.0 * sixth(wide_row)
    lane_of = sixth(wide_lane)
    lane_in = wide_lane.astype(F32) - 6.0 * lane_of
    spread = nn(own, (row_in == lane_in).astype(F32), HIGH)
    spread = jnp.where(row_in == lane_of, spread, 0.0)
    fold = (
        sixth(iota((frames, cam_cols), 1)) == iota((frames, cam_cols), 0).astype(F32)
    ).astype(F32)
    out_diag[...] = nn(fold, spread, HIGH)[:, 0:36]

    for rel in range(1, n_edge):
        meta_copy(rel).wait_send()
        edge_copy(rel).wait_send()
        for s in range(slots):
            feat_copy(rel, s).wait_send()
    for rel in range(1, n_tile):
        tile_copy(rel).wait_send()
    each(n_edge * slots, lambda k: sent_pair(txt_up(k), txt_dn(k)))

    def sent(e):
        sent_pair(hid_up(e), hid_dn(e))
        sent_pair(row_up(mext, s_mup, r_mup, e), row_dn(mext, s_mdn, r_mdn, e))
        sent_pair(row_up(rext, s_rup, r_rup, e), row_dn(rext, s_rdn, r_rdn, e))

    each(edges, sent)


def per_device(
    features,
    hidden_state,
    edge_source,
    edge_owner,
    edge_target,
    edge_counts,
    corr_weight,
    gate_weight,
    candidate_weight,
    jacobian_weight,
    confidence_weight,
):
    n_edge, n_tile = lax.axis_size("edge"), lax.axis_size("tile")
    edges = hidden_state.shape[0]
    frames, rows, width, chan = features.shape
    slots = max(2, (2 * edges + n_edge - 1) // n_edge)
    band = rows * width
    me = lax.axis_index("edge")
    owners = edge_owner[:, 0]

    numbers = jnp.concatenate([owners, edge_target, edge_source, edge_counts])
    numbers = jnp.pad(numbers, (0, 128 - numbers.shape[0]))
    inner = jnp.arange(16)[None, :]
    frame = jnp.where(
        inner < 6, (me * frames + edge_source)[:, None], (owners * frames + edge_target)[:, None]
    )
    spots = jnp.where(inner < 12, frame * 6 + inner % 6, -1).reshape(-1)
    spots = jnp.pad(spots, (0, 128 - spots.shape[0]), constant_values=-1)
    meta = jnp.stack([numbers, spots]).astype(jnp.int32)

    grid = corr_weight.reshape(WINDOW, WINDOW, chan)
    side = 32 - RADIUS
    rest = width - side - WINDOW
    corr_w = jnp.stack(
        [
            jnp.pad(grid, ((0, 1), (side, rest), (0, 0))).reshape(8 * width, chan),
            jnp.pad(grid, ((1, 0), (side, rest), (0, 0))).reshape(8 * width, chan),
        ]
    )
    corr_w = jnp.roll(corr_w.reshape(2, 4, 2 * width, chan), width // 2 - 1, axis=2)
    corr_w = corr_w.reshape(2, 8 * width, chan)
    gap = jnp.zeros((chan, 104), BF)
    head_w = jnp.concatenate(
        [
            jacobian_weight,
            gap,
            jnp.broadcast_to(confidence_weight[:, 0:1], (chan, 12)),
            jnp.broadcast_to(confidence_weight[:, 1:2], (chan, 12)),
            gap,
        ],
        axis=1,
    )
    dims = (n_edge, n_tile, edges, frames, rows, width, slots)
    total_slots = n_edge * slots
    text_rows = rows + 2 * RADIUS
    text_rows = text_rows + text_rows % 2
    ext = band + 2 * width
    dma = pltpu.SemaphoreType.DMA
    vmem = pl.BlockSpec(memory_space=pltpu.VMEM)
    hidden_next, cam, diag = pl.pallas_call(
        functools.partial(kernel, dims),
        out_shape=(
            jax.ShapeDtypeStruct((edges, band, chan), BF),
            jax.ShapeDtypeStruct((frames * n_edge * 6 // n_tile, frames * 6), F32),
            jax.ShapeDtypeStruct((frames, 36), F32),
        ),
        in_specs=[vmem] * 7,
        out_specs=(vmem, vmem, vmem),
        scratch_shapes=[
            pltpu.VMEM((n_edge, 2, 128), jnp.int32),
            pltpu.SMEM((n_edge, 2, 128), jnp.int32),
            pltpu.VMEM(((n_edge - 1) * slots, band, chan), BF),
            pltpu.VMEM((total_slots, text_rows * width, chan), BF),
            pltpu.VMEM((edges, band, chan), BF),
            pltpu.VMEM((edges, ext, chan), BF),
            pltpu.VMEM((edges, ext, chan), BF),
            pltpu.VMEM((edges, ext, chan), BF),
            pltpu.VMEM((ext, 3 * chan), BF),
            pltpu.VMEM((9 * chan, 2 * chan), BF),
            pltpu.VMEM((9 * chan, 3 * chan), BF),
            pltpu.VMEM((9 * chan, chan), BF),
            pltpu.VMEM((edges, band, 2 * chan), F32),
            pltpu.VMEM((edges, band, chan), F32),
            pltpu.VMEM((edges, band, chan), F32),
            pltpu.VMEM((16, 128), F32),
            pltpu.VMEM((n_tile, 16, 128), F32),
            pltpu.VMEM((16, 128), F32),
            pltpu.VMEM((n_edge, 16, 128), F32),
            dma((n_edge,)),
            dma((n_edge,)),
            dma,
            dma((total_slots,)),
            dma((total_slots,)),
        ]
        + [dma((total_slots,))] * 4
        + [dma((edges,))] * 12
        + [dma((n_tile,)), dma((n_tile,)), dma((n_edge,)), dma((n_edge,))],
        compiler_params=pltpu.CompilerParams(
            collective_id=0, has_side_effects=True, vmem_limit_bytes=56 * 1024 * 1024
        ),
    )(
        meta,
        features.reshape(frames, band, chan),
        hidden_state.reshape(edges, band, chan),
        corr_w,
        gate_weight,
        candidate_weight,
        head_w,
    )
    return hidden_next.reshape(hidden_state.shape), cam, diag


def solution(mesh):
    placed = (
        P("edge", "tile", None, None),
        P("edge", "tile", None, None),
        P("edge"),
        P("edge", None),
        P("edge"),
        P("edge"),
        P(),
        P(),
        P(),
        P(),
        P(),
    )
    return jax.shard_map(
        per_device,
        mesh=mesh,
        in_specs=placed,
        out_specs=(P("edge", "tile", None, None), P("tile", "edge"), P("edge", None)),
        check_vma=False,
    )
```

time: 206 us -> 83.5 us (0.41)
  Pallas kernels: 0 us -> 70.7 us
  blocking collectives: 38.4 us -> 0 us
  other arithmetic: 36.9 us -> 2.91 us
  starting transfers between devices: 31.5 us -> 0 us
  waiting for transfers between devices: 28.7 us -> 0 us
  matrix products: 26.1 us -> 0 us
  local copies, waits for them, and re-layouts: 27.6 us -> 8.21 us
  between operations: 15.6 us -> 1.33 us
    pallas_call x0 -> x1, Pallas kernels: none -> 70.7 us  [per_device(): pl.pallas_call(functools.partial(kernel, dims), out_shape=(jax.ShapeDtype...]
    psum x1 -> x0, blocking collectives: 28.7 us -> none  [per_device(): pose_diagonal = lax.psum(diagonal_part, 'tile')]
    dot_general x25 -> x0, matrix products: 26.1 us -> none  [the longest x18 20.2 us: convolve(): jnp.einsum('erwc,ck->erwk', window, weight[row_step, col_step], preferred...]
    unnamed x4 -> x0, other arithmetic: 22.3 us -> none
    all_to_all x3 -> x0, waiting for transfers between devices: 19.9 us -> none  [the longest x1 15.4 us: per_device(): lax.all_to_all(asked, 'edge', split_axis=0, concat_axis=0, tiled=True)]
    ppermute x6 -> x0, starting transfers between devices: 19.8 us -> none  [the longest x3 15.7 us: padded_2(): lax.ppermute(tail, axis, [(i, (i + 1) % count) for i in range(ends)])]
    another operation x50 -> x1, local copies, waits for them, and re-layouts: 16 us -> 0.01 us  [per_device(): meta = jnp.stack([numbers, spots]).astype(jnp.int32)]
    all_to_all x3 -> x0, starting transfers between devices: 11.7 us -> none  [the longest x1 4.33 us: per_device(): lax.all_to_all(asked, 'edge', split_axis=0, concat_axis=0, tiled=True)]
  transfers between devices with their start and end apart: 10 -> 0, of which waited for: 6 -> 0; matrix products, arithmetic and copies ran while one was open for 4% -> 0% of each run, Pallas kernels for 0% -> 0%
where the time goes in v1:
time: 83.5 us; the launch traced here: 83.1 us
  Pallas kernels  70.7 us (85%)
  local copies, waits for them, and re-layouts  8.21 us (10%)
  other arithmetic  2.91 us (3%)
  between operations  1.33 us (2%)
    pallas_call x1, Pallas kernels, per_device(): pl.pallas_call(functools.partial(kernel, dims), out_shape=(jax.ShapeDtype...  70.7 us
    unnamed x4, local copies, waits for them, and re-layouts  5.7 us

profile of v1, /device:TPU:0, one launch (start us, length us, event | category | flops | bytes accessed | tf_op | source)
XLA Modules:
  0.0 83.1 jit_solution(1650123533879234592)
XLA Ops:
  1.3 0.8 pad_add_fusion.1
  2.1 0.7 multiply_add_fusion
  2.8 0.7 slice_bitcast_fusion
  3.5 0.1 add_select_fusion
  3.6 0.1 select_n.41
  3.7 0.6 pad_add_fusion.meta_in
  4.2 0.7 reshape.120
  5.0 0.1 broadcast_in_dim.65
  5.0 0.1 broadcast_in_dim.63
  5.1 0.8 copy.14
  6.0 0.8 concatenate.13.head_w
  6.8 0.8 fusion
  7.5 70.7 %shard_map.130 = (bf16[8,384,128]{2,1,0:T(8,128)(2,1)}, f32[72,144]{1,0:T(8,128)}, f32[24,36]{1,0:T(8,128)}) custom-call(s32[2,128]{1,0:T(2,128)} %pad_add_fusion.meta_in, bf16[24,384,128]{2,1,0:T(8,128)(2,1)} %bitcast.14, bf16[8,384,128]{2,1,0:T(8,128)(2,1)} %bitcast.17, bf16[2,512,128]{2,1,0:T(8,128)(2,1)} %bitcast.15, bf16[3,3,256,256]{3,2,1,0:T(8,128)(2,1)} %gate_w.1, ...), custom_call_target="tpu_custom_call" | custom-call | tf_op jit(solution)/shard_map/pallas_call | solution.py:551
  78.2 2.1 %copy.19 = bf16[8,6,64,128]{3,2,1,0:T(8,128)(2,1)} copy(bf16[8,6,64,128]{3,2,1,0:T(8,128)(2,1)} %bitcast.16) | data formatting | bytes 1572864
  80.3 1.5 %copy.20 = f32[72,144]{1,0:T(8,128)} copy(f32[72,144]{1,0:T(8,128)} %get-tuple-element.21) | data formatting | bytes 82944
  81.8 1.3 %copy.21 = f32[24,36]{1,0:T(8,128)} copy(f32[24,36]{1,0:T(8,128)} %get-tuple-element.22) | data formatting | bytes 6912
  (5 shorter events, 0.1 us)

commit v2 on v1

--- a/solution.py
+++ b/solution.py
@@ -39,16 +39,20 @@
 def kernel(
     dims,
     meta_in,
-    feat,
-    hidden,
-    corr_w,
+    feat_h,
+    hidden_h,
+    corr_in,
     gate_w,
     cand_w,
-    head_w,
+    jac_in,
+    conf_in,
     out_hidden,
-    out_cam,
-    out_diag,
+    gall,
     meta_all,
+    feat,
+    corr_w,
+    jall,
+    wall,
     meta_s,
     send,
     text,
@@ -66,7 +70,8 @@
     gpart,
     gtile,
     gsum,
-    gall,
+    l_in,
+    l_w,
     s_meta,
     r_meta,
     l_meta,
@@ -101,6 +106,26 @@
     up, down = tile - 1, tile + 1
     has_up, has_down = tile > 0, tile < n_tile - 1
 
+    loads = [
+        pltpu.make_async_copy(feat_h, feat, l_in.at[0]),
+        pltpu.make_async_copy(hidden_h, hext.at[:, pl.ds(width, band)], l_in.at[1]),
+    ]
+    fills = []
+    for a in range(3):
+        for b in range(3):
+            at = pl.ds((a * 3 + b) * 128, 128)
+            first, second = pl.ds(0, 128), pl.ds(128, 128)
+            pairs = (
+                (gate_w.at[a, b, first], wh.at[at]),
+                (gate_w.at[a, b, second], wm.at[at, pl.ds(0, 256)]),
+                (cand_w.at[a, b, second], wm.at[at, pl.ds(256, 128)]),
+                (cand_w.at[a, b, first], wr.at[at]),
+            )
+            for source, target in pairs:
+                fills.append(pltpu.make_async_copy(source, target, l_w.at[len(fills)]))
+    for load in loads + fills:
+        load.start()
+
     barrier = pltpu.get_barrier_semaphore()
     for rel in range(1, n_edge):
         pl.semaphore_signal(
@@ -132,13 +157,13 @@
 
     def hid_up(e):
         return remote(
-            hidden.at[e, pl.ds(0, width)], hext.at[e, pl.ds(width + band, width)],
+            hidden_h.at[e, pl.ds(0, width)], hext.at[e, pl.ds(width + band, width)],
             s_hup.at[e], r_hup.at[e], me, up,
         )
 
     def hid_dn(e):
         return remote(
-            hidden.at[e, pl.ds(band - width, width)], hext.at[e, pl.ds(0, width)],
+            hidden_h.at[e, pl.ds(band - width, width)], hext.at[e, pl.ds(0, width)],
             s_hdn.at[e], r_hdn.at[e], me, down,
         )
 
@@ -237,6 +262,34 @@
             text[k, pl.ds(band + 2 * halo, width)] = zero_row
 
         each(n_edge * slots, clear_pad)
+
+    spot = iota((2 * width, 64), 0)
+    rank = ((spot + 97) & 63) - 32
+    second = ((spot + 97) & 127) >> 6
+    names = iota((2 * width, 64), 1)
+    lookup = jnp.concatenate(
+        [corr_in[...].astype(F32), jnp.zeros((64 - WINDOW * WINDOW, 128), F32)], axis=0
+    ).astype(BF)
+    for par in range(2):
+        for g in range(4):
+            down_by = 2 * g - par + second
+            fits = (rank >= -RADIUS) & (rank <= RADIUS) & (down_by >= 0) & (down_by < WINDOW)
+            pick = (names == down_by * WINDOW + rank + RADIUS) & fits
+            corr_w[par, pl.ds(g * 2 * width, 2 * width)] = nn(
+                pick.astype(F32).astype(BF), lookup
+            ).astype(BF)
+
+    place12 = iota((32, 64), 0)
+    which = place12 >> 4
+    within = place12 & 15
+    name12 = iota((32, 64), 1)
+    pick_j = (within < 12) & (name12 == which * 12 + within)
+    pick_c = (within < 12) & (name12 == 24 + which)
+    both_heads = jnp.concatenate(
+        [jac_in[...].astype(F32), conf_in[...].astype(F32), jnp.zeros((32, 128), F32)], axis=0
+    ).astype(BF)
+    picks_all = jnp.concatenate([pick_j.astype(F32), pick_c.astype(F32)], axis=0).astype(BF)
+    head_w = nn(picks_all, both_heads).astype(BF)
 
     meta_all[me] = meta_in[...]
     for rel in range(1, n_edge):
@@ -244,6 +297,7 @@
             meta_in, meta_all.at[(me - rel + n_edge) % n_edge], s_meta.at[rel], r_meta.at[rel],
             (me + rel) % n_edge, tile,
         ).wait_recv()
+    loads[0].wait()
     local = pltpu.make_async_copy(meta_all, meta_s, l_meta)
     local.start()
     local.wait()
@@ -279,14 +333,6 @@
         text[s, pl.ds(halo, band)] = feat[asks[0][s]]
     for s in range(slots):
         start_pair(txt_up(s), txt_dn(s))
-
-    for a in range(3):
-        for b in range(3):
-            at = pl.ds((a * 3 + b) * 128, 128)
-            wh[at, :] = gate_w[a, b, 0:128, :]
-            wm[at, 0:256] = gate_w[a, b, 128:256, :]
-            wm[at, 256:384] = cand_w[a, b, 128:256, :]
-            wr[at, :] = cand_w[a, b, 0:128, :]
 
     col = iota((band + 2 * width, 128), 0) & (width - 1)
 
@@ -321,10 +367,12 @@
             sref[e, pl.ds(first * width, last - first * width)] = flipped(
                 source[first * width : last]
             )
-        hext[e, pl.ds(width, band)] = hidden[e]
         recv_pair(hid_up(e), hid_dn(e))
         gpre[e] = nn(shifted(hext, e), wh[...])
 
+    loads[1].wait()
+    for fill in fills:
+        fill.wait()
     each(edges, state_part)
 
     for s in range(slots):
@@ -377,36 +425,36 @@
         cpre[e] = both[:, 256:384]
         gate = jax.nn.sigmoid(gpre[e] + both[:, 0:256])
         upd[e] = gate[:, 0:128]
-        rext[e, pl.ds(width, band)] = (gate[:, 128:256] * hidden[e].astype(F32)).astype(BF)
+        rext[e, pl.ds(width, band)] = (gate[:, 128:256] * hext[e, pl.ds(width, band)].astype(F32)).astype(BF)
         start_pair(row_up(rext, s_rup, r_rup, e), row_dn(rext, s_rdn, r_rdn, e))
 
     each(edges, gates)
-
-    gpart[...] = jnp.zeros_like(gpart)
-    lane16 = iota((16, 128), 1)
-    row16 = iota((16, 128), 0)
 
     def finish(e):
         recv_pair(row_up(rext, s_rup, r_rup, e), row_dn(rext, s_rdn, r_rdn, e))
         candidate = jnp.tanh(cpre[e] + nn(shifted(rext, e), wr[...]))
         update = upd[e]
-        state = hidden[e]
+        state = hext[e, pl.ds(width, band)]
         fresh = ((1.0 - update) * state.astype(F32) + update * candidate).astype(BF)
         used = (e < meta_s[me, 0, 24]).astype(F32)
         live = jnp.full((band, 128), used) > 0.5
         out_hidden[e] = jnp.where(live, fresh, state)
-        heads = nn(fresh, head_w[...])
-        jac = heads[:, 0:128]
-        weighted = jac * jax.nn.softplus(heads[:, 128:256])
-        square = lax.dot_general(
-            weighted, jac, (((0,), (0,)), ((), ())), preferred_element_type=F32, precision=HIGH
-        )
-        other = pltpu.roll(pltpu.roll(square, 116, 0), 116, 1)
-        block = (square + other)[0:16] * (used / (MAPH * width))
-        block = jnp.where((lane16 < 12) & (row16 < 12), block, 0.0)
-        gpart[...] += pltpu.roll(block, e * 16, 1)
+        heads = nt(head_w, fresh)
+        jac = heads[0:32]
+        weighted = jac * jax.nn.softplus(heads[32:64])
+        at16 = pl.ds(pl.multiple_of(e * 16, 16), 16)
+        jall[at16] = jnp.concatenate([jac[0:16], jac[16:32]], axis=1).astype(BF)
+        wall[at16] = jnp.concatenate([weighted[0:16], weighted[16:32]], axis=1).astype(BF)
 
     each(edges, finish)
+
+    same = (iota((128, 128), 0) >> 4) == (iota((128, 128), 1) >> 4)
+    square = jnp.where(same, nt(wall[...], jall[...]), 0.0)
+    blocks = square[0:16]
+    for e in range(1, edges):
+        blocks = blocks + square[e * 16 : (e + 1) * 16]
+    alive = (iota((16, 128), 1) >> 4) < meta_s[me, 0, 24]
+    gpart[...] = jnp.where(alive, blocks * (1.0 / (MAPH * width)), 0.0)
 
     def tile_copy(rel):
         return remote(
@@ -438,19 +486,63 @@
             (me + rel) % n_edge, tile,
         ).wait_recv()
 
+    for rel in range(1, n_edge):
+        meta_copy(rel).wait_send()
+        edge_copy(rel).wait_send()
+        for s in range(slots):
+            feat_copy(rel, s).wait_send()
+    for rel in range(1, n_tile):
+        tile_copy(rel).wait_send()
+    each(n_edge * slots, lambda k: sent_pair(txt_up(k), txt_dn(k)))
+
+    def sent(e):
+        sent_pair(hid_up(e), hid_dn(e))
+        sent_pair(row_up(mext, s_mup, r_mup, e), row_dn(mext, s_mdn, r_mdn, e))
+        sent_pair(row_up(rext, s_rup, r_rup, e), row_dn(rext, s_rdn, r_rdn, e))
+
+    each(edges, sent)
+
+
+def halves(value):
+    high = value.astype(BF)
+    return high, (value - high.astype(F32)).astype(BF)
+
+
+def assemble(dims, meta_s, gall, hidden_h, out_hidden, out_cam, out_diag, held, sem):
+    n_edge, n_tile, edges, frames, rows, width, slots = dims
+    fetch = pltpu.make_async_copy(hidden_h, held, sem.at[0])
+    fetch.start()
+    me = lax.axis_index("edge")
+    tile = lax.axis_index("tile")
     cam_rows, cam_cols = out_cam.shape
     row_id = iota((cam_rows, 128), 0) + tile * cam_rows
     col_id = iota((cam_cols, 128), 0) + me * cam_cols
     same = (iota((128, 128), 0) >> 4) == (iota((128, 128), 1) >> 4)
-    lefts, rights = [], []
+    lane = iota((1, 128), 1)
+    inner = lane & 15
+    digit = jnp.where(inner < 6, inner, inner - 6)
+    lefts, lows, rights = [], [], []
     for j in range(n_edge):
-        spots = meta_all[j, 1:2, :]
+        spots = jnp.full((1, 128), -1, jnp.int32)
+        for e in range(edges):
+            source = (j * frames + meta_s[j, 0, 16 + e]) * 6
+            target = (meta_s[j, 0, e] * frames + meta_s[j, 0, 8 + e]) * 6
+            here = jnp.where(inner < 6, source, target) + digit
+            spots = jnp.where(((lane >> 4) == e) & (inner < 12), here, spots)
         mine = (col_id == spots).astype(F32)
-        left = jnp.concatenate([(row_id == spots).astype(F32), mine], axis=0)
-        stack = jnp.concatenate([gall[j]] * 8, axis=0)
-        lefts.append(nn(left, jnp.where(same, stack, 0.0), HIGH))
-        rights.append(mine)
-    placed = nt(jnp.concatenate(lefts, axis=1), jnp.concatenate(rights, axis=1), HIGH)
+        left = jnp.concatenate([(row_id == spots).astype(F32), mine], axis=0).astype(BF)
+        stack = jnp.where(same, jnp.concatenate([gall[j]] * 8, axis=0), 0.0)
+        picked = nn(
+            jnp.concatenate([left, left], axis=1), jnp.concatenate(halves(stack), axis=0)
+        )
+        high, low = halves(picked)
+        lefts.append(high)
+        lows.append(low)
+        rights.append(mine.astype(BF))
+    placed = nt(jnp.concatenate(lefts + lows, axis=1), jnp.concatenate(rights + rights, axis=1))
+    fetch.wait()
+    store = pltpu.make_async_copy(held, out_hidden, sem.at[1])
+    store.start()
     cam = placed[0:cam_rows]
     row_frame = sixth(iota((cam_rows, cam_cols), 0) + tile * cam_rows)
     col_frame = sixth(iota((cam_rows, cam_cols), 1) + me * cam_cols)
@@ -464,28 +556,15 @@
     row_in = wide_row.astype(F32) - 6.0 * sixth(wide_row)
     lane_of = sixth(wide_lane)
     lane_in = wide_lane.astype(F32) - 6.0 * lane_of
-    spread = nn(own, (row_in == lane_in).astype(F32), HIGH)
-    spread = jnp.where(row_in == lane_of, spread, 0.0)
+    gather = (row_in == lane_in).astype(F32).astype(BF)
+    high, low = halves(own)
+    spread = jnp.where(row_in == lane_of, nn(high, gather) + nn(low, gather), 0.0)
     fold = (
         sixth(iota((frames, cam_cols), 1)) == iota((frames, cam_cols), 0).astype(F32)
-    ).astype(F32)
-    out_diag[...] = nn(fold, spread, HIGH)[:, 0:36]
-
-    for rel in range(1, n_edge):
-        meta_copy(rel).wait_send()
-        edge_copy(rel).wait_send()
-        for s in range(slots):
-            feat_copy(rel, s).wait_send()
-    for rel in range(1, n_tile):
-        tile_copy(rel).wait_send()
-    each(n_edge * slots, lambda k: sent_pair(txt_up(k), txt_dn(k)))
-
-    def sent(e):
-        sent_pair(hid_up(e), hid_dn(e))
-        sent_pair(row_up(mext, s_mup, r_mup, e), row_dn(mext, s_mdn, r_mdn, e))
-        sent_pair(row_up(rext, s_rup, r_rup, e), row_dn(rext, s_rdn, r_rdn, e))
-
-    each(edges, sent)
+    ).astype(F32).astype(BF)
+    high, low = halves(spread)
+    out_diag[...] = (nn(fold, high) + nn(fold, low))[:, 0:36]
+    store.wait()
 
 
 def per_device(
@@ -506,41 +585,11 @@
     frames, rows, width, chan = features.shape
     slots = max(2, (2 * edges + n_edge - 1) // n_edge)
     band = rows * width
-    me = lax.axis_index("edge")
     owners = edge_owner[:, 0]
 
     numbers = jnp.concatenate([owners, edge_target, edge_source, edge_counts])
     numbers = jnp.pad(numbers, (0, 128 - numbers.shape[0]))
-    inner = jnp.arange(16)[None, :]
-    frame = jnp.where(
-        inner < 6, (me * frames + edge_source)[:, None], (owners * frames + edge_target)[:, None]
-    )
-    spots = jnp.where(inner < 12, frame * 6 + inner % 6, -1).reshape(-1)
-    spots = jnp.pad(spots, (0, 128 - spots.shape[0]), constant_values=-1)
-    meta = jnp.stack([numbers, spots]).astype(jnp.int32)
-
-    grid = corr_weight.reshape(WINDOW, WINDOW, chan)
-    side = 32 - RADIUS
-    rest = width - side - WINDOW
-    corr_w = jnp.stack(
-        [
-            jnp.pad(grid, ((0, 1), (side, rest), (0, 0))).reshape(8 * width, chan),
-            jnp.pad(grid, ((1, 0), (side, rest), (0, 0))).reshape(8 * width, chan),
-        ]
-    )
-    corr_w = jnp.roll(corr_w.reshape(2, 4, 2 * width, chan), width // 2 - 1, axis=2)
-    corr_w = corr_w.reshape(2, 8 * width, chan)
-    gap = jnp.zeros((chan, 104), BF)
-    head_w = jnp.concatenate(
-        [
-            jacobian_weight,
-            gap,
-            jnp.broadcast_to(confidence_weight[:, 0:1], (chan, 12)),
-            jnp.broadcast_to(confidence_weight[:, 1:2], (chan, 12)),
-            gap,
-        ],
-        axis=1,
-    )
+    meta = numbers[None, :].astype(jnp.int32)
     dims = (n_edge, n_tile, edges, frames, rows, width, slots)
     total_slots = n_edge * slots
     text_rows = rows + 2 * RADIUS
@@ -548,18 +597,22 @@
     ext = band + 2 * width
     dma = pltpu.SemaphoreType.DMA
     vmem = pl.BlockSpec(memory_space=pltpu.VMEM)
-    hidden_next, cam, diag = pl.pallas_call(
+    hbm = pl.BlockSpec(memory_space=pl.ANY)
+    state, gall, meta_all = pl.pallas_call(
         functools.partial(kernel, dims),
         out_shape=(
             jax.ShapeDtypeStruct((edges, band, chan), BF),
-            jax.ShapeDtypeStruct((frames * n_edge * 6 // n_tile, frames * 6), F32),
-            jax.ShapeDtypeStruct((frames, 36), F32),
+            jax.ShapeDtypeStruct((n_edge, 16, 128), F32),
+            jax.ShapeDtypeStruct((n_edge, 1, 128), jnp.int32),
         ),
-        in_specs=[vmem] * 7,
+        in_specs=[vmem, hbm, hbm, vmem, hbm, hbm, vmem, vmem],
         out_specs=(vmem, vmem, vmem),
         scratch_shapes=[
-            pltpu.VMEM((n_edge, 2, 128), jnp.int32),
-            pltpu.SMEM((n_edge, 2, 128), jnp.int32),
+            pltpu.VMEM((frames, band, chan), BF),
+            pltpu.VMEM((2, 8 * width, chan), BF),
+            pltpu.VMEM((edges * 16, 2 * band), BF),
+            pltpu.VMEM((edges * 16, 2 * band), BF),
+            pltpu.SMEM((n_edge, 1, 128), jnp.int32),
             pltpu.VMEM(((n_edge - 1) * slots, band, chan), BF),
             pltpu.VMEM((total_slots, text_rows * width, chan), BF),
             pltpu.VMEM((edges, band, chan), BF),
@@ -576,7 +629,8 @@
             pltpu.VMEM((16, 128), F32),
             pltpu.VMEM((n_tile, 16, 128), F32),
             pltpu.VMEM((16, 128), F32),
-            pltpu.VMEM((n_edge, 16, 128), F32),
+            dma((2,)),
+            dma((36,)),
             dma((n_edge,)),
             dma((n_edge,)),
             dma,
@@ -593,11 +647,23 @@
         meta,
         features.reshape(frames, band, chan),
         hidden_state.reshape(edges, band, chan),
-        corr_w,
+        corr_weight,
         gate_weight,
         candidate_weight,
-        head_w,
+        jacobian_weight.T,
+        jnp.pad(confidence_weight.T, ((0, 6), (0, 0))),
     )
+    hidden_next, cam, diag = pl.pallas_call(
+        functools.partial(assemble, dims),
+        out_shape=(
+            jax.ShapeDtypeStruct((edges, band, chan), BF),
+            jax.ShapeDtypeStruct((frames * n_edge * 6 // n_tile, frames * 6), F32),
+            jax.ShapeDtypeStruct((frames, 36), F32),
+        ),
+        in_specs=[pl.BlockSpec(memory_space=pltpu.SMEM), vmem, hbm],
+        out_specs=(hbm, vmem, vmem),
+        scratch_shapes=[pltpu.VMEM((edges, band, chan), BF), dma((2,))],
+    )(meta_all, gall, state)
     return hidden_next.reshape(hidden_state.shape), cam, diag
 
 

time: 83.5 us -> 68.5 us (0.82)
  local copies, waits for them, and re-layouts: 8.21 us -> 1.75 us
  Pallas kernels: 70.7 us -> 64.4 us
  other arithmetic: 2.91 us -> 0.77 us
    pallas_call x1, Pallas kernels: 70.7 us -> 60.9 us  [per_device(): pl.pallas_call(functools.partial(kernel, dims), out_shape=(jax.ShapeDtype...]
    unnamed x4 -> x0, local copies, waits for them, and re-layouts: 5.7 us -> none
    pallas_call x0 -> x1, Pallas kernels: none -> 3.55 us  [per_device(): pl.pallas_call(functools.partial(assemble, dims), out_shape=(jax.ShapeDty...]
    pad x1, local copies, waits for them, and re-layouts: 0.04 us -> 1.24 us  [per_device(): jnp.pad(confidence_weight.T, ((0, 6), (0, 0)))]
where the time goes in v2:
time: 68.5 us; the launch traced here: 68.2 us
  Pallas kernels  64.4 us (94%)
  local copies, waits for them, and re-layouts  1.75 us (3%)
  between operations  1.29 us (2%)
  other arithmetic  0.77 us (1%)
    pallas_call x1, Pallas kernels, per_device(): pl.pallas_call(functools.partial(kernel, dims), out_shape=(jax.ShapeDtype...  60.9 us
    pallas_call x1, Pallas kernels, per_device(): pl.pallas_call(functools.partial(assemble, dims), out_shape=(jax.ShapeDty...  3.55 us

profile of v2, /device:TPU:0, one launch (start us, length us, event | category | flops | bytes accessed | tf_op | source)
XLA Modules:
  0.0 68.2 jit_solution(2589964178528870347)
XLA Ops:
  1.3 0.8 %pad_add_fusion = s32[25]{0:T(128)S(1)} fusion(s32[1]{0:T(128)S(6)} %copy.14, s32[8]{0:T(128)} %param.13, s32[8]{0:T(128)} %param.15, s32[8]{0:T(128)} %bitcast.11), kind=kLoop, calls=%fused_computation | loop fusion | flops 75 | bytes 200 | tf_op jit(solution)/shard_map/concatenate | solution.py:590
  2.0 0.5 pad_bitcast_fusion.meta_in
  2.6 1.2 %pad.9.conf_in = bf16[8,128]{1,0:T(8,128)(2,1)} pad(bf16[2,128]{1,0:T(2,128)(2,1)} %bitcast.12, bf16[]{:T(256)} %constant.3.clone.1), padding=0_6x0_0 | pad | bytes 2562 | tf_op jit(solution)/shard_map/jit(_pad)/pad | solution.py:654
  3.8 60.9 %shard_map.130 = (bf16[8,384,128]{2,1,0:T(8,128)(2,1)}, f32[4,16,128]{2,1,0:T(8,128)}, s32[4,1,128]{2,1,0:T(1,128)}) custom-call(s32[1,128]{1,0:T(1,128)} %pad_bitcast_fusion.meta_in, bf16[24,384,128]{2,1,0:T(8,128)(2,1)} %bitcast.8, bf16[8,384,128]{2,1,0:T(8,128)(2,1)} %bitcast.9, bf16[49,128]{1,0:T(8,128)(2,1)} %corr_in.1, ...), custom_call_target="tpu_custom_call" | custom-call | tf_op jit(solution)/shard_map/pallas_call | solution.py:601
  64.7 3.5 %shard_map.131 = (bf16[8,384,128]{2,1,0:T(8,128)(2,1)}, f32[72,144]{1,0:T(8,128)}, f32[24,36]{1,0:T(8,128)}) custom-call(s32[4,1,128]{2,1,0:T(1,128)} %get-tuple-element.9.meta_s, f32[4,16,128]{2,1,0:T(8,128)} %get-tuple-element.10.gall, bf16[8,384,128]{2,1,0:T(8,128)(2,1)} %get-tuple-element.11.hidden_h), custom_call_target="tpu_custom_call" | custom-call | tf_op jit(solution)/shard_map/pallas_call | solution.py:656

commit v3 on v2

--- a/solution.py
+++ b/solution.py
@@ -284,12 +284,23 @@
     within = place12 & 15
     name12 = iota((32, 64), 1)
     pick_j = (within < 12) & (name12 == which * 12 + within)
-    pick_c = (within < 12) & (name12 == 24 + which)
-    both_heads = jnp.concatenate(
-        [jac_in[...].astype(F32), conf_in[...].astype(F32), jnp.zeros((32, 128), F32)], axis=0
+    padded_jac = jnp.concatenate(
+        [jac_in[...].astype(F32), jnp.zeros((40, 128), F32)], axis=0
     ).astype(BF)
-    picks_all = jnp.concatenate([pick_j.astype(F32), pick_c.astype(F32)], axis=0).astype(BF)
-    head_w = nn(picks_all, both_heads).astype(BF)
+    conf_wide = conf_in[...].astype(F32)
+    tall = iota((32, 128), 0)
+    conf_rows = jnp.where(
+        tall < 16,
+        jnp.broadcast_to(conf_wide[0:1], (32, 128)),
+        jnp.broadcast_to(conf_wide[1:2], (32, 128)),
+    )
+    head_w = jnp.concatenate(
+        [
+            nn(pick_j.astype(F32).astype(BF), padded_jac),
+            jnp.where((tall & 15) < 12, conf_rows, 0.0),
+        ],
+        axis=0,
+    ).astype(BF)
 
     meta_all[me] = meta_in[...]
     for rel in range(1, n_edge):
@@ -336,19 +347,30 @@
 
     col = iota((band + 2 * width, 128), 0) & (width - 1)
 
-    def shifted(buf, e):
-        value = buf[e]
-        wide = value.astype(F32)
-        left = jnp.where(col == 0, 0.0, pltpu.roll(wide, 1, 0)).astype(BF)
-        right = jnp.where(
-            col == width - 1, 0.0, pltpu.roll(wide, band + 2 * width - 1, 0)
-        ).astype(BF)
-        x3[:, 0:128] = left
-        x3[:, 128:256] = value
-        x3[:, 256:384] = right
-        return jnp.concatenate(
-            [x3[0:band], x3[width : width + band], x3[2 * width : 2 * width + band]], axis=1
-        )
+    group = 2 if edges % 2 == 0 else 1
+
+    def shifted(buf, first):
+        parts = []
+        for q in range(group):
+            value = buf[first + q]
+            wide = value.astype(F32)
+            left = jnp.where(col == 0, 0.0, pltpu.roll(wide, 1, 0)).astype(BF)
+            right = jnp.where(
+                col == width - 1, 0.0, pltpu.roll(wide, band + 2 * width - 1, 0)
+            ).astype(BF)
+            x3[q, :, 0:128] = left
+            x3[q, :, 128:256] = value
+            x3[q, :, 256:384] = right
+        for q in range(group):
+            parts.append(
+                jnp.concatenate(
+                    [x3[q, a * width : a * width + band] for a in range(3)], axis=1
+                )
+            )
+        return jnp.concatenate(parts, axis=0)
+
+    def grouped(body):
+        each(edges // group, lambda i: body(i * group))
 
     flip_row, flip_col = iota((2 * width, 2 * width), 0), iota((2 * width, 2 * width), 1)
     flip = (
@@ -361,19 +383,23 @@
         return nn(flip[0:count, 0:count], value).astype(BF)
 
     def state_part(e):
-        source = feat[meta_s[me, 0, 16 + e]]
-        for first in range(0, rows, 2):
-            last = min(rows, first + 2) * width
-            sref[e, pl.ds(first * width, last - first * width)] = flipped(
-                source[first * width : last]
-            )
-        recv_pair(hid_up(e), hid_dn(e))
-        gpre[e] = nn(shifted(hext, e), wh[...])
+        for q in range(group):
+            recv_pair(hid_up(e + q), hid_dn(e + q))
+        for q in range(group):
+            source = feat[meta_s[me, 0, 16 + e + q]]
+            for first in range(0, rows, 2):
+                last = min(rows, first + 2) * width
+                sref[e + q, pl.ds(first * width, last - first * width)] = flipped(
+                    source[first * width : last]
+                )
+        value = nn(shifted(hext, e), wh[...])
+        for q in range(group):
+            gpre[e + q] = value[q * band : (q + 1) * band]
 
     loads[1].wait()
     for fill in fills:
         fill.wait()
-    each(edges, state_part)
+    grouped(state_part)
 
     for s in range(slots):
         for rel in range(1, n_edge):
@@ -393,7 +419,7 @@
             rank = rank + jnp.where((meta_s[me, 0, k] == mine) & (k < e), 1, 0)
         return ((mine - me + n_edge) % n_edge) * slots + jnp.minimum(rank, slots - 1)
 
-    def motion(e):
+    def motion_of(e):
         k = slot_of(e)
         source = sref[e]
         target = text[k]
@@ -415,38 +441,59 @@
             mext[e, pl.ds((first + 1) * width, count * width)] = flipped(
                 jnp.concatenate(values, axis=0)
             )
-        start_pair(row_up(mext, s_mup, r_mup, e), row_dn(mext, s_mdn, r_mdn, e))
-
-    each(edges, motion)
+
+    def motion(e):
+        for q in range(group):
+            motion_of(e + q)
+        for q in range(group):
+            start_pair(
+                row_up(mext, s_mup, r_mup, e + q), row_dn(mext, s_mdn, r_mdn, e + q)
+            )
+
+    grouped(motion)
 
     def gates(e):
-        recv_pair(row_up(mext, s_mup, r_mup, e), row_dn(mext, s_mdn, r_mdn, e))
+        for q in range(group):
+            recv_pair(
+                row_up(mext, s_mup, r_mup, e + q), row_dn(mext, s_mdn, r_mdn, e + q)
+            )
         both = nn(shifted(mext, e), wm[...])
-        cpre[e] = both[:, 256:384]
-        gate = jax.nn.sigmoid(gpre[e] + both[:, 0:256])
-        upd[e] = gate[:, 0:128]
-        rext[e, pl.ds(width, band)] = (gate[:, 128:256] * hext[e, pl.ds(width, band)].astype(F32)).astype(BF)
-        start_pair(row_up(rext, s_rup, r_rup, e), row_dn(rext, s_rdn, r_rdn, e))
-
-    each(edges, gates)
+        for q in range(group):
+            part = both[q * band : (q + 1) * band]
+            cpre[e + q] = part[:, 256:384]
+            gate = jax.nn.sigmoid(gpre[e + q] + part[:, 0:256])
+            upd[e + q] = gate[:, 0:128]
+            state = hext[e + q, pl.ds(width, band)].astype(F32)
+            rext[e + q, pl.ds(width, band)] = (gate[:, 128:256] * state).astype(BF)
+        for q in range(group):
+            start_pair(
+                row_up(rext, s_rup, r_rup, e + q), row_dn(rext, s_rdn, r_rdn, e + q)
+            )
+
+    grouped(gates)
 
     def finish(e):
-        recv_pair(row_up(rext, s_rup, r_rup, e), row_dn(rext, s_rdn, r_rdn, e))
-        candidate = jnp.tanh(cpre[e] + nn(shifted(rext, e), wr[...]))
-        update = upd[e]
-        state = hext[e, pl.ds(width, band)]
-        fresh = ((1.0 - update) * state.astype(F32) + update * candidate).astype(BF)
-        used = (e < meta_s[me, 0, 24]).astype(F32)
-        live = jnp.full((band, 128), used) > 0.5
-        out_hidden[e] = jnp.where(live, fresh, state)
-        heads = nt(head_w, fresh)
-        jac = heads[0:32]
-        weighted = jac * jax.nn.softplus(heads[32:64])
-        at16 = pl.ds(pl.multiple_of(e * 16, 16), 16)
-        jall[at16] = jnp.concatenate([jac[0:16], jac[16:32]], axis=1).astype(BF)
-        wall[at16] = jnp.concatenate([weighted[0:16], weighted[16:32]], axis=1).astype(BF)
-
-    each(edges, finish)
+        for q in range(group):
+            recv_pair(
+                row_up(rext, s_rup, r_rup, e + q), row_dn(rext, s_rdn, r_rdn, e + q)
+            )
+        mixed = nn(shifted(rext, e), wr[...])
+        for q in range(group):
+            candidate = jnp.tanh(cpre[e + q] + mixed[q * band : (q + 1) * band])
+            update = upd[e + q]
+            state = hext[e + q, pl.ds(width, band)]
+            fresh = ((1.0 - update) * state.astype(F32) + update * candidate).astype(BF)
+            used = (e + q < meta_s[me, 0, 24]).astype(F32)
+            live = jnp.full((band, 128), used) > 0.5
+            out_hidden[e + q] = jnp.where(live, fresh, state)
+            heads = nt(head_w, fresh)
+            jac = heads[0:32]
+            weighted = jac * jax.nn.softplus(heads[32:64])
+            at16 = pl.ds(pl.multiple_of((e + q) * 16, 16), 16)
+            jall[at16] = jnp.concatenate([jac[0:16], jac[16:32]], axis=1).astype(BF)
+            wall[at16] = jnp.concatenate([weighted[0:16], weighted[16:32]], axis=1).astype(BF)
+
+    grouped(finish)
 
     same = (iota((128, 128), 0) >> 4) == (iota((128, 128), 1) >> 4)
     square = jnp.where(same, nt(wall[...], jall[...]), 0.0)
@@ -587,9 +634,10 @@
     band = rows * width
     owners = edge_owner[:, 0]
 
-    numbers = jnp.concatenate([owners, edge_target, edge_source, edge_counts])
-    numbers = jnp.pad(numbers, (0, 128 - numbers.shape[0]))
-    meta = numbers[None, :].astype(jnp.int32)
+    fields = ((owners, 0), (edge_target, 8), (edge_source, 16), (edge_counts, 24))
+    meta = jnp.zeros((1, 128), jnp.int32)
+    for field, at in fields:
+        meta = meta + jnp.pad(field, (at, 128 - at - field.shape[0]))[None, :]
     dims = (n_edge, n_tile, edges, frames, rows, width, slots)
     total_slots = n_edge * slots
     text_rows = rows + 2 * RADIUS
@@ -619,7 +667,7 @@
             pltpu.VMEM((edges, ext, chan), BF),
             pltpu.VMEM((edges, ext, chan), BF),
             pltpu.VMEM((edges, ext, chan), BF),
-            pltpu.VMEM((ext, 3 * chan), BF),
+            pltpu.VMEM((2, ext, 3 * chan), BF),
             pltpu.VMEM((9 * chan, 2 * chan), BF),
             pltpu.VMEM((9 * chan, 3 * chan), BF),
             pltpu.VMEM((9 * chan, chan), BF),
@@ -651,7 +699,7 @@
         gate_weight,
         candidate_weight,
         jacobian_weight.T,
-        jnp.pad(confidence_weight.T, ((0, 6), (0, 0))),
+        confidence_weight.T,
     )
     hidden_next, cam, diag = pl.pallas_call(
         functools.partial(assemble, dims),

time: 68.5 us -> 65.7 us (0.959)
  local copies, waits for them, and re-layouts: 1.75 us -> 0 us
  Pallas kernels: 64.4 us -> 62.9 us
    pallas_call x1, Pallas kernels: 60.9 us -> 59.3 us  [per_device(): pl.pallas_call(functools.partial(kernel, dims), out_shape=(jax.ShapeDtype...]
    add x0 -> x1, other arithmetic: none -> 1.28 us  [per_device(): meta = meta + jnp.pad(field, (at, 128 - at - field.shape[0]))[None, :]]
    pad x1 -> x0, local copies, waits for them, and re-layouts: 1.24 us -> none  [per_device(): jnp.pad(confidence_weight.T, ((0, 6), (0, 0)))]
    concatenate x1 -> x0, other arithmetic: 0.77 us -> none  [per_device(): numbers = jnp.concatenate([owners, edge_target, edge_source, edge_counts])]
where the time goes in v3:
time: 65.7 us; the launch traced here: 65.4 us
  Pallas kernels  62.9 us (96%)
  between operations  1.29 us (2%)
  other arithmetic  1.28 us (2%)
    pallas_call x1, Pallas kernels, per_device(): pl.pallas_call(functools.partial(kernel, dims), out_shape=(jax.ShapeDtype...  59.3 us
    pallas_call x1, Pallas kernels, per_device(): pl.pallas_call(functools.partial(assemble, dims), out_shape=(jax.ShapeDty...  3.55 us

profile of v3, /device:TPU:0, one launch (start us, length us, event | category | flops | bytes accessed | tf_op | source)
XLA Modules:
  0.0 65.4 jit_solution(13380208317977638907)
XLA Ops:
  1.3 1.3 %add_bitcast_fusion.meta_in = s32[1,128]{1,0:T(1,128)} fusion(s32[1]{0:T(128)S(6)} %copy.14, s32[8]{0:T(128)} %param.13, s32[8]{0:T(128)} %param.15, s32[8]{0:T(128)} %bitcast.12), kind=kLoop, calls=%fused_computation | loop fusion | flops 384 | bytes 612 | tf_op jit(solution)/shard_map/add | solution.py:640
  2.6 59.3 %shard_map.130 = (bf16[8,384,128]{2,1,0:T(8,128)(2,1)}, f32[4,16,128]{2,1,0:T(8,128)}, s32[4,1,128]{2,1,0:T(1,128)}) custom-call(s32[1,128]{1,0:T(1,128)} %add_bitcast_fusion.meta_in, bf16[24,384,128]{2,1,0:T(8,128)(2,1)} %bitcast.8, bf16[8,384,128]{2,1,0:T(8,128)(2,1)} %bitcast.9, bf16[49,128]{1,0:T(8,128)(2,1)} %corr_in.1, ...), custom_call_target="tpu_custom_call" | custom-call | tf_op jit(solution)/shard_map/pallas_call | solution.py:649
  61.9 3.5 %shard_map.131 = (bf16[8,384,128]{2,1,0:T(8,128)(2,1)}, f32[72,144]{1,0:T(8,128)}, f32[24,36]{1,0:T(8,128)}) custom-call(s32[4,1,128]{2,1,0:T(1,128)} %get-tuple-element.9.meta_s, f32[4,16,128]{2,1,0:T(8,128)} %get-tuple-element.10.gall, bf16[8,384,128]{2,1,0:T(8,128)(2,1)} %get-tuple-element.11.hidden_h), custom_call_target="tpu_custom_call" | custom-call | tf_op jit(solution)/shard_map/pallas_call | solution.py:704

commit v4 on v3

--- a/solution.py
+++ b/solution.py
@@ -50,6 +50,8 @@
     gall,
     meta_all,
     feat,
+    held,
+    l_out,
     corr_w,
     jall,
     wall,
@@ -263,6 +265,49 @@
 
         each(n_edge * slots, clear_pad)
 
+    meta_all[me] = meta_in[...]
+    for rel in range(1, n_edge):
+        remote(
+            meta_in, meta_all.at[(me - rel + n_edge) % n_edge], s_meta.at[rel], r_meta.at[rel],
+            (me + rel) % n_edge, tile,
+        ).wait_recv()
+    loads[0].wait()
+    local = pltpu.make_async_copy(meta_all, meta_s, l_meta)
+    local.start()
+    local.wait()
+
+    def asked(peer):
+        picks = [jnp.int32(0)] * slots
+        rank = jnp.int32(0)
+        for k in range(edges):
+            hit = (meta_s[peer, 0, k] == me).astype(jnp.int32)
+            goal = meta_s[peer, 0, 8 + k]
+            for s in range(slots):
+                picks[s] = jnp.where((hit == 1) & (rank == s), goal, picks[s])
+            rank = rank + hit
+        return picks
+
+    def feat_copy(rel, s):
+        return remote(
+            send.at[(rel - 1) * slots + s],
+            text.at[rel * slots + s, pl.ds(halo, band)],
+            s_feat.at[rel * slots + s],
+            r_feat.at[rel * slots + s],
+            (me - rel + n_edge) % n_edge,
+            tile,
+        )
+
+    asks = [asked((me - rel + n_edge) % n_edge) for rel in range(n_edge)]
+    for s in range(slots):
+        for rel in range(1, n_edge):
+            send[(rel - 1) * slots + s] = feat[asks[rel][s]]
+        for rel in range(1, n_edge):
+            feat_copy(rel, s).start()
+    for s in range(slots):
+        text[s, pl.ds(halo, band)] = feat[asks[0][s]]
+    for s in range(slots):
+        start_pair(txt_up(s), txt_dn(s))
+
     spot = iota((2 * width, 64), 0)
     rank = ((spot + 97) & 63) - 32
     second = ((spot + 97) & 127) >> 6
@@ -302,49 +347,6 @@
         axis=0,
     ).astype(BF)
 
-    meta_all[me] = meta_in[...]
-    for rel in range(1, n_edge):
-        remote(
-            meta_in, meta_all.at[(me - rel + n_edge) % n_edge], s_meta.at[rel], r_meta.at[rel],
-            (me + rel) % n_edge, tile,
-        ).wait_recv()
-    loads[0].wait()
-    local = pltpu.make_async_copy(meta_all, meta_s, l_meta)
-    local.start()
-    local.wait()
-
-    def asked(peer):
-        picks = [jnp.int32(0)] * slots
-        rank = jnp.int32(0)
-        for k in range(edges):
-            hit = (meta_s[peer, 0, k] == me).astype(jnp.int32)
-            goal = meta_s[peer, 0, 8 + k]
-            for s in range(slots):
-                picks[s] = jnp.where((hit == 1) & (rank == s), goal, picks[s])
-            rank = rank + hit
-        return picks
-
-    def feat_copy(rel, s):
-        return remote(
-            send.at[(rel - 1) * slots + s],
-            text.at[rel * slots + s, pl.ds(halo, band)],
-            s_feat.at[rel * slots + s],
-            r_feat.at[rel * slots + s],
-            (me - rel + n_edge) % n_edge,
-            tile,
-        )
-
-    asks = [asked((me - rel + n_edge) % n_edge) for rel in range(n_edge)]
-    for s in range(slots):
-        for rel in range(1, n_edge):
-            send[(rel - 1) * slots + s] = feat[asks[rel][s]]
-        for rel in range(1, n_edge):
-            feat_copy(rel, s).start()
-    for s in range(slots):
-        text[s, pl.ds(halo, band)] = feat[asks[0][s]]
-    for s in range(slots):
-        start_pair(txt_up(s), txt_dn(s))
-
     col = iota((band + 2 * width, 128), 0) & (width - 1)
 
     group = 2 if edges % 2 == 0 else 1
@@ -485,7 +487,7 @@
             fresh = ((1.0 - update) * state.astype(F32) + update * candidate).astype(BF)
             used = (e + q < meta_s[me, 0, 24]).astype(F32)
             live = jnp.full((band, 128), used) > 0.5
-            out_hidden[e + q] = jnp.where(live, fresh, state)
+            held[e + q] = jnp.where(live, fresh, state)
             heads = nt(head_w, fresh)
             jac = heads[0:32]
             weighted = jac * jax.nn.softplus(heads[32:64])
@@ -494,6 +496,8 @@
             wall[at16] = jnp.concatenate([weighted[0:16], weighted[16:32]], axis=1).astype(BF)
 
     grouped(finish)
+    store = pltpu.make_async_copy(held, out_hidden, l_out)
+    store.start()
 
     same = (iota((128, 128), 0) >> 4) == (iota((128, 128), 1) >> 4)
     square = jnp.where(same, nt(wall[...], jall[...]), 0.0)
@@ -533,6 +537,7 @@
             (me + rel) % n_edge, tile,
         ).wait_recv()
 
+    store.wait()
     for rel in range(1, n_edge):
         meta_copy(rel).wait_send()
         edge_copy(rel).wait_send()
@@ -654,9 +659,11 @@
             jax.ShapeDtypeStruct((n_edge, 1, 128), jnp.int32),
         ),
         in_specs=[vmem, hbm, hbm, vmem, hbm, hbm, vmem, vmem],
-        out_specs=(vmem, vmem, vmem),
+        out_specs=(hbm, vmem, vmem),
         scratch_shapes=[
             pltpu.VMEM((frames, band, chan), BF),
+            pltpu.VMEM((edges, band, chan), BF),
+            dma,
             pltpu.VMEM((2, 8 * width, chan), BF),
             pltpu.VMEM((edges * 16, 2 * band), BF),
             pltpu.VMEM((edges * 16, 2 * band), BF),

time: 65.7 us -> 65.6 us (level)
  no operation moved by 1% of the time
where the time goes in v4:
time: 65.6 us; the launch traced here: 65.3 us
  Pallas kernels  62.7 us (96%)
  between operations  1.29 us (2%)
  other arithmetic  1.28 us (2%)
    pallas_call x1, Pallas kernels, per_device(): pl.pallas_call(functools.partial(kernel, dims), out_shape=(jax.ShapeDtype...  59.1 us
    pallas_call x1, Pallas kernels, per_device(): pl.pallas_call(functools.partial(assemble, dims), out_shape=(jax.ShapeDty...  3.55 us

profile of v4, /device:TPU:0, one launch (start us, length us, event | category | flops | bytes accessed | tf_op | source)
XLA Modules:
  0.0 65.3 jit_solution(6009093044678636430)
XLA Ops:
  1.3 1.3 %add_bitcast_fusion.meta_in = s32[1,128]{1,0:T(1,128)} fusion(s32[1]{0:T(128)S(6)} %copy.14, s32[8]{0:T(128)} %param.13, s32[8]{0:T(128)} %param.15, s32[8]{0:T(128)} %bitcast.12), kind=kLoop, calls=%fused_computation | loop fusion | flops 384 | bytes 612 | tf_op jit(solution)/shard_map/add | solution.py:645
  2.6 59.1 %shard_map.130 = (bf16[8,384,128]{2,1,0:T(8,128)(2,1)}, f32[4,16,128]{2,1,0:T(8,128)}, s32[4,1,128]{2,1,0:T(1,128)}) custom-call(s32[1,128]{1,0:T(1,128)} %add_bitcast_fusion.meta_in, bf16[24,384,128]{2,1,0:T(8,128)(2,1)} %bitcast.8, bf16[8,384,128]{2,1,0:T(8,128)(2,1)} %bitcast.9, bf16[49,128]{1,0:T(8,128)(2,1)} %corr_in.1, ...), custom_call_target="tpu_custom_call" | custom-call | tf_op jit(solution)/shard_map/pallas_call | solution.py:654
  61.7 3.5 %shard_map.131 = (bf16[8,384,128]{2,1,0:T(8,128)(2,1)}, f32[72,144]{1,0:T(8,128)}, f32[24,36]{1,0:T(8,128)}) custom-call(s32[4,1,128]{2,1,0:T(1,128)} %get-tuple-element.9.meta_s, f32[4,16,128]{2,1,0:T(8,128)} %get-tuple-element.10.gall, bf16[8,384,128]{2,1,0:T(8,128)(2,1)} %get-tuple-element.11.hidden_h), custom_call_target="tpu_custom_call" | custom-call | tf_op jit(solution)/shard_map/pallas_call | solution.py:711
